TPU v7x, 128 devices: a whole 4x4x4 slice. The times are simulated.
128 devices in a mesh: section: 8 (over x, core), tensor: 16 (over z, y).
Axes of the slice: x: 4, y: 4, z: 4, core: 2. Of those that a mesh axis runs over, the one named last changes fastest.
Arguments:
- hidden_in: bfloat16 [64, 2560], P(None, 'tensor'), may hold values from -6 to 6
- pre_gain: float32 [8, 2560], P('section'), may hold values from 0.1 to 1.9
- w_zx: bfloat16 [8, 2560, 80, 128], P('section', None, 'tensor'), may hold values from -0.125 to 0.125
- w_bc: bfloat16 [8, 2560, 256], P('section'), may hold values from -0.125 to 0.125
- w_dt: bfloat16 [8, 2560, 80], P('section', None, 'tensor'), may hold values from -0.125 to 0.125
- dt_bias: float32 [8, 80], P('section', 'tensor'), may hold values from -4 to -1
- a_log: float32 [8, 80], P('section', 'tensor'), may hold values from 0 to 2.77
- d_skip: float32 [8, 80], P('section', 'tensor'), may hold values from 0.5 to 2
- conv_x_weight: float32 [8, 4, 80, 64], P('section', None, 'tensor'), may hold values from -3 to 3
- conv_x_bias: float32 [8, 80, 64], P('section', 'tensor'), may hold values from -3 to 3
- conv_bc_weight: float32 [8, 4, 256], P('section'), may hold values from -3 to 3
- conv_bc_bias: float32 [8, 256], P('section'), may hold values from -3 to 3
- inner_gain: float32 [8, 80, 64], P('section', 'tensor'), may hold values from 0.1 to 1.9
- w_out: bfloat16 [8, 80, 64, 2560], P('section', 'tensor'), may hold values from -0.078125 to 0.078125
- conv_x_state: bfloat16 [8, 64, 3, 80, 64], P('section', None, None, 'tensor'), may hold values from -6 to 6
- conv_bc_state: bfloat16 [8, 64, 3, 256], P('section'), may hold values from -6 to 6
- ssm_state: bfloat16 [8, 64, 80, 64, 128], P('section', None, 'tensor'), may hold values from -14 to 14
Outputs:
- section_hidden: bfloat16 [8, 64, 2560], P('section', None, 'tensor')
- conv_x_new: bfloat16 [8, 64, 3, 80, 64], P('section', None, None, 'tensor')
- conv_bc_new: bfloat16 [8, 64, 3, 256], P('section')
- ssm_new: bfloat16 [8, 64, 80, 64, 128], P('section', None, 'tensor')
All inputs are finite; a program needn't handle non-finite values.
Results may differ from a plain program's by a relative error of at most 0.02.
Values may be sent and summed in bfloat16 or wider, within the bound.
A program may use at most 64 MiB of HBM per device.

v0:
```python
import jax
import jax.numpy as jnp
from jax import lax
from jax.sharding import PartitionSpec as P

epsilon = 1e-05


def copy_for_each(array, axis):
    size = lax.axis_size(axis)
    return lax.all_to_all(
        jnp.broadcast_to(array[None], (size, *array.shape)), axis, 0, 0, tiled=True
    )


def in_order(parts, dim):
    parts = jnp.moveaxis(parts, 0, dim)
    lengths = parts.shape
    return parts.reshape(*lengths[:dim], lengths[dim] * lengths[dim + 1], *lengths[dim + 2 :])


def collect(array, axis, dim):
    parts = copy_for_each(array, axis)
    return in_order(parts, dim)


def of_everyone(array, axis):
    return copy_for_each(array, axis).sum(axis=0)


def in_one(arrays, axis):
    ends = [0]
    for a in arrays:
        ends.append(ends[-1] + a.size)
    running = of_everyone(jnp.concatenate([a.ravel() for a in arrays]), axis)
    return tuple((running[b:e].reshape(a.shape) for a, b, e in zip(arrays, ends, ends[1:])))


def shifted(value, axis, steps):
    count = lax.axis_size(axis)
    leading, last = (max(0, -steps), min(count, count - steps))
    return lax.ppermute(value, axis, [(source, source + steps) for source in range(leading, last)])


def mixer_core(
    normed,
    w_zx,
    w_bc,
    w_dt,
    dt_bias,
    a_log,
    d_skip,
    conv_x_weight,
    conv_x_bias,
    conv_bc_weight,
    conv_bc_bias,
    conv_x_state,
    conv_bc_state,
    ssm_state,
):
    row_count = normed.shape[0]
    model_width = w_zx.shape[0]
    head_count = w_zx.shape[1]
    head_size = w_zx.shape[2] // 2
    state_size = w_bc.shape[1] // 2
    both_parts = jnp.dot(
        normed,
        w_zx.reshape(model_width, head_count * 2 * head_size),
        preferred_element_type=jnp.float32,
    )
    both_parts = both_parts.reshape(row_count, head_count, 2 * head_size)
    gate_z = both_parts[:, :, :head_size]
    x_fresh = both_parts[:, :, head_size:].astype(jnp.bfloat16)
    bc_fresh = jnp.dot(normed, w_bc, preferred_element_type=jnp.float32).astype(jnp.bfloat16)
    dt_raw = jnp.dot(normed, w_dt, preferred_element_type=jnp.float32)
    x_window = jnp.concatenate([conv_x_state, x_fresh[:, None]], axis=1)
    bc_window = jnp.concatenate([conv_bc_state, bc_fresh[:, None]], axis=1)
    x_conv = jax.nn.silu(
        jnp.sum(x_window.astype(jnp.float32) * conv_x_weight[None], axis=1) + conv_x_bias[None]
    )
    bc_conv = jax.nn.silu(
        jnp.sum(bc_window.astype(jnp.float32) * conv_bc_weight[None], axis=1) + conv_bc_bias[None]
    )
    b_input = bc_conv[:, :state_size]
    c_output = bc_conv[:, state_size:]
    step_size = jax.nn.softplus(dt_raw + dt_bias[None])
    decay_rate = jnp.exp(-step_size * jnp.exp(a_log)[None])
    state_f = (
        decay_rate[:, :, None, None] * ssm_state.astype(jnp.float32)
        + (step_size[:, :, None] * x_conv)[:, :, :, None] * b_input[:, None, None, :]
    )
    y_out = jnp.sum(state_f * c_output[:, None, None, :], axis=-1) + d_skip[None, :, None] * x_conv
    gated_out = y_out * jax.nn.silu(gate_z)
    return (gated_out, x_window[:, 1:], bc_window[:, 1:], state_f.astype(jnp.bfloat16))


def put_rows(buffer, which_layer, row_start, fresh, older, is_live):
    chosen = jnp.where(is_live, fresh, older)
    corner = [jnp.zeros((), jnp.int32) + which_layer, row_start] + [jnp.zeros((), jnp.int32)] * (
        buffer.ndim - 2
    )
    return lax.dynamic_update_slice(buffer, chosen[None], tuple(corner))


def shards(
    hidden_in,
    pre_gain,
    w_zx,
    w_bc,
    w_dt,
    dt_bias,
    a_log,
    d_skip,
    conv_x_weight,
    conv_x_bias,
    conv_bc_weight,
    conv_bc_bias,
    inner_gain,
    w_out,
    conv_x_state,
    conv_bc_state,
    ssm_state,
):
    section_count = lax.axis_size("section")
    tensor_count = lax.axis_size("tensor")
    section_at = lax.axis_index("section")
    tensor_at = lax.axis_index("tensor")
    stream_count = hidden_in.shape[0]
    share_cols = hidden_in.shape[1]
    block_rows = stream_count // section_count
    tick_count = section_count + section_count - 1
    source = collect(hidden_in, "tensor", 1)
    carried_cols = source.shape[1]

    def advance(moment, carry):
        incoming, conv_x_buf, conv_bc_buf, ssm_buf, section_buf = carry
        which_block = moment - section_at
        is_live = jnp.logical_and(which_block >= 0, which_block < section_count)
        row_start = jnp.clip(which_block, 0, section_count - 1) * block_rows
        first_rows = lax.dynamic_slice_in_dim(source, row_start, block_rows, 0)
        current = jnp.where(section_at == 0, first_rows, incoming)
        conv_x_old = lax.dynamic_slice_in_dim(conv_x_buf[0], row_start, block_rows, 0)
        conv_bc_old = lax.dynamic_slice_in_dim(conv_bc_buf[0], row_start, block_rows, 0)
        ssm_old = lax.dynamic_slice_in_dim(ssm_buf[0], row_start, block_rows, 0)
        whole_rows = current
        wide = whole_rows.astype(jnp.float32)
        normed = (
            wide
            * lax.rsqrt(jnp.mean(wide * wide, axis=-1, keepdims=True) + epsilon)
            * pre_gain[0][None]
        ).astype(jnp.bfloat16)
        gated_out, conv_x_next, conv_bc_next, ssm_next = mixer_core(
            normed,
            w_zx[0],
            w_bc[0],
            w_dt[0],
            dt_bias[0],
            a_log[0],
            d_skip[0],
            conv_x_weight[0],
            conv_x_bias[0],
            conv_bc_weight[0],
            conv_bc_bias[0],
            conv_x_old,
            conv_bc_old,
            ssm_old,
        )
        local_squares = jnp.sum(gated_out * gated_out, axis=(1, 2))
        channel_total = gated_out.shape[1] * gated_out.shape[2] * tensor_count
        scaled_inner = (gated_out * inner_gain[0][None]).astype(jnp.bfloat16)
        local_heads = scaled_inner.shape[1] * scaled_inner.shape[2]
        partial_value = jnp.dot(
            scaled_inner.reshape(block_rows, local_heads),
            w_out[0].reshape(local_heads, w_out.shape[-1]),
            preferred_element_type=jnp.float32,
        )
        summed, summed_squares = in_one((partial_value, local_squares), "tensor")
        factor = lax.rsqrt(summed_squares / channel_total + epsilon)[:, None]
        current = (current.astype(jnp.float32) + summed * factor).astype(jnp.bfloat16)
        conv_x_buf = put_rows(conv_x_buf, 0, row_start, conv_x_next, conv_x_old, is_live)
        conv_bc_buf = put_rows(conv_bc_buf, 0, row_start, conv_bc_next, conv_bc_old, is_live)
        ssm_buf = put_rows(ssm_buf, 0, row_start, ssm_next, ssm_old, is_live)
        own_share = lax.dynamic_slice_in_dim(current, tensor_at * share_cols, share_cols, 1)
        outgoing = shifted(current, "section", 1)
        section_old = lax.dynamic_slice_in_dim(section_buf[0], row_start, block_rows, 0)
        section_buf = put_rows(section_buf, 0, row_start, own_share, section_old, is_live)
        return (outgoing, conv_x_buf, conv_bc_buf, ssm_buf, section_buf)

    start_carry = (
        jnp.zeros((block_rows, carried_cols), jnp.bfloat16),
        conv_x_state,
        conv_bc_state,
        ssm_state,
        jnp.zeros((1, stream_count, share_cols), jnp.bfloat16),
    )
    final_carry = lax.fori_loop(0, tick_count, advance, start_carry)
    return (final_carry[4], final_carry[1], final_carry[2], final_carry[3])


def solution(mesh):
    placed = (
        P(None, "tensor"),
        P("section", None),
        P("section", None, "tensor", None),
        P("section", None, None),
        P("section", None, "tensor"),
        P("section", "tensor"),
        P("section", "tensor"),
        P("section", "tensor"),
        P("section", None, "tensor", None),
        P("section", "tensor", None),
        P("section", None, None),
        P("section", None),
        P("section", "tensor", None),
        P("section", "tensor", None, None),
        P("section", None, None, "tensor", None),
        P("section", None, None, None),
        P("section", None, "tensor", None, None),
    )
    return jax.shard_map(
        shards,
        mesh=mesh,
        in_specs=placed,
        out_specs=(
            P("section", None, "tensor"),
            P("section", None, None, "tensor", None),
            P("section", None, None, None),
            P("section", None, "tensor", None, None),
        ),
        check_vma=False,
    )
```

profile of v0, /device:TPU:1, one launch (start us, length us, event | category | flops | bytes accessed | tf_op | source)
XLA Modules:
  0.0 682.5 jit_solution(8601275566412019550)
XLA Ops:
  3.8 6.1 copy.116
  10.8 8.6 %all-to-all-start.1 = ((bf16[16,64,160]{2,1,0:T(8,128)(2,1)}), bf16[16,64,160]{2,1,0:T(8,128)(2,1)S(1)}, u32[]{:S(2)}, u32[]{:S(2)}) async-start(bf16[16,64,160]{2,1,0:T(8,128)(2,1)} %broadcast_in_dim.100), calls=%async_computation.1 | async-start | bytes 1048576 | tf_op jit(solution)/shard_map/all_to_all | solution.py:11
  20.6 5.6 copy.72
  26.3 3.6 all-to-all-done.1
  31.5 651.0 %while.23 = (s32[]{:T(128)}, bf16[8,2560]{1,0:T(8,128)(2,1)S(1)}, bf16[1,64,3,5,64]{4,1,3,2,0:T(8,128)(2,1)}, bf16[1,64,3,256]{3,1,2,0:T(8,128)(2,1)}, bf16[1,64...) while((s32[]{:T(128)}, bf16[8,2560]{1,0:T(8,128)(2,1)S(1)}, ...), condition=%wide.region_7.8_spmd, body=%wide.region_0.7_spmd.sunk | while | flops 54887680 | bytes 16769857 | solution.py:196
  37.3 2.9 fusion.71
  45.4 3.7 all-to-all-start
  53.5 13.5 %all-to-all-done = f32[16,1,20488]{2,1,0:T(1,128)S(1)} async-done(((f32[16,1,20488]{2,1,0:T(1,128)}), f32[16,1,20488]{2,1,0:T(1,128)S(1)}, u32[]{:S(2)}, u32[]{:S(2)}) %all-to-all-start) | async-done | bytes 1311264 | tf_op jit(solution)/shard_map/while/body/eval_jaxpr/all_to_all | solution.py:11
  67.9 6.7 collective-permute-start
  81.4 2.9 fusion.71
  89.5 3.7 all-to-all-start
  95.2 2.4 fusion.81
  97.6 15.4 %all-to-all-done = f32[16,1,20488]{2,1,0:T(1,128)S(1)} async-done(((f32[16,1,20488]{2,1,0:T(1,128)}), f32[16,1,20488]{2,1,0:T(1,128)S(1)}, u32[]{:S(2)}, u32[]{:S(2)}) %all-to-all-start) | async-done | bytes 1311264 | tf_op jit(solution)/shard_map/while/body/eval_jaxpr/all_to_all | solution.py:11
  113.9 5.1 collective-permute-start
  125.8 2.9 fusion.71
  133.9 3.7 all-to-all-start
  139.6 2.4 fusion.81
  142.0 14.1 %all-to-all-done = f32[16,1,20488]{2,1,0:T(1,128)S(1)} async-done(((f32[16,1,20488]{2,1,0:T(1,128)}), f32[16,1,20488]{2,1,0:T(1,128)S(1)}, u32[]{:S(2)}, u32[]{:S(2)}) %all-to-all-start) | async-done | bytes 1311264 | tf_op jit(solution)/shard_map/while/body/eval_jaxpr/all_to_all | solution.py:11
  157.0 6.0 collective-permute-start
  169.8 2.9 fusion.71
  177.9 3.7 all-to-all-start
  183.6 2.4 fusion.81
  186.0 13.4 %all-to-all-done = f32[16,1,20488]{2,1,0:T(1,128)S(1)} async-done(((f32[16,1,20488]{2,1,0:T(1,128)}), f32[16,1,20488]{2,1,0:T(1,128)S(1)}, u32[]{:S(2)}, u32[]{:S(2)}) %all-to-all-start) | async-done | bytes 1311264 | tf_op jit(solution)/shard_map/while/body/eval_jaxpr/all_to_all | solution.py:11
  200.3 5.5 collective-permute-start
  212.6 2.9 fusion.71
  220.7 3.7 all-to-all-start
  226.4 2.4 fusion.81
  228.8 13.6 %all-to-all-done = f32[16,1,20488]{2,1,0:T(1,128)S(1)} async-done(((f32[16,1,20488]{2,1,0:T(1,128)}), f32[16,1,20488]{2,1,0:T(1,128)S(1)}, u32[]{:S(2)}, u32[]{:S(2)}) %all-to-all-start) | async-done | bytes 1311264 | tf_op jit(solution)/shard_map/while/body/eval_jaxpr/all_to_all | solution.py:11
  243.4 5.2 collective-permute-start
  255.4 2.9 fusion.71
  263.6 3.7 all-to-all-start
  271.6 13.9 %all-to-all-done = f32[16,1,20488]{2,1,0:T(1,128)S(1)} async-done(((f32[16,1,20488]{2,1,0:T(1,128)}), f32[16,1,20488]{2,1,0:T(1,128)S(1)}, u32[]{:S(2)}, u32[]{:S(2)}) %all-to-all-start) | async-done | bytes 1311264 | tf_op jit(solution)/shard_map/while/body/eval_jaxpr/all_to_all | solution.py:11
  286.4 5.0 collective-permute-start
  298.2 2.9 fusion.71
  306.4 3.7 all-to-all-start
  312.0 2.4 fusion.81
  314.4 14.2 %all-to-all-done = f32[16,1,20488]{2,1,0:T(1,128)S(1)} async-done(((f32[16,1,20488]{2,1,0:T(1,128)}), f32[16,1,20488]{2,1,0:T(1,128)S(1)}, u32[]{:S(2)}, u32[]{:S(2)}) %all-to-all-start) | async-done | bytes 1311264 | tf_op jit(solution)/shard_map/while/body/eval_jaxpr/all_to_all | solution.py:11
  329.6 4.6 collective-permute-start
  341.1 2.9 fusion.71
  349.2 3.7 all-to-all-start
  357.2 14.8 %all-to-all-done = f32[16,1,20488]{2,1,0:T(1,128)S(1)} async-done(((f32[16,1,20488]{2,1,0:T(1,128)}), f32[16,1,20488]{2,1,0:T(1,128)S(1)}, u32[]{:S(2)}, u32[]{:S(2)}) %all-to-all-start) | async-done | bytes 1311264 | tf_op jit(solution)/shard_map/while/body/eval_jaxpr/all_to_all | solution.py:11
  372.9 4.1 collective-permute-start
  383.9 2.9 fusion.71
  392.0 3.7 all-to-all-start
  400.0 15.5 %all-to-all-done = f32[16,1,20488]{2,1,0:T(1,128)S(1)} async-done(((f32[16,1,20488]{2,1,0:T(1,128)}), f32[16,1,20488]{2,1,0:T(1,128)S(1)}, u32[]{:S(2)}, u32[]{:S(2)}) %all-to-all-start) | async-done | bytes 1311264 | tf_op jit(solution)/shard_map/while/body/eval_jaxpr/all_to_all | solution.py:11
  416.4 3.4 collective-permute-start
  426.7 2.9 fusion.71
  434.8 3.7 all-to-all-start
  442.8 17.1 %all-to-all-done = f32[16,1,20488]{2,1,0:T(1,128)S(1)} async-done(((f32[16,1,20488]{2,1,0:T(1,128)}), f32[16,1,20488]{2,1,0:T(1,128)S(1)}, u32[]{:S(2)}, u32[]{:S(2)}) %all-to-all-start) | async-done | bytes 1311264 | tf_op jit(solution)/shard_map/while/body/eval_jaxpr/all_to_all | solution.py:11
  469.7 2.9 fusion.71
  477.8 3.7 all-to-all-start
  485.9 17.7 %all-to-all-done = f32[16,1,20488]{2,1,0:T(1,128)S(1)} async-done(((f32[16,1,20488]{2,1,0:T(1,128)}), f32[16,1,20488]{2,1,0:T(1,128)S(1)}, u32[]{:S(2)}, u32[]{:S(2)}) %all-to-all-start) | async-done | bytes 1311264 | tf_op jit(solution)/shard_map/while/body/eval_jaxpr/all_to_all | solution.py:11
  513.4 2.9 fusion.71
  521.5 3.7 all-to-all-start
  529.6 17.7 %all-to-all-done = f32[16,1,20488]{2,1,0:T(1,128)S(1)} async-done(((f32[16,1,20488]{2,1,0:T(1,128)}), f32[16,1,20488]{2,1,0:T(1,128)S(1)}, u32[]{:S(2)}, u32[]{:S(2)}) %all-to-all-start) | async-done | bytes 1311264 | tf_op jit(solution)/shard_map/while/body/eval_jaxpr/all_to_all | solution.py:11
  557.1 2.9 fusion.71
  565.2 3.7 all-to-all-start
  573.3 17.7 %all-to-all-done = f32[16,1,20488]{2,1,0:T(1,128)S(1)} async-done(((f32[16,1,20488]{2,1,0:T(1,128)}), f32[16,1,20488]{2,1,0:T(1,128)S(1)}, u32[]{:S(2)}, u32[]{:S(2)}) %all-to-all-start) | async-done | bytes 1311264 | tf_op jit(solution)/shard_map/while/body/eval_jaxpr/all_to_all | solution.py:11
  600.8 2.9 fusion.71
  608.9 3.7 all-to-all-start
  617.0 17.7 %all-to-all-done = f32[16,1,20488]{2,1,0:T(1,128)S(1)} async-done(((f32[16,1,20488]{2,1,0:T(1,128)}), f32[16,1,20488]{2,1,0:T(1,128)S(1)}, u32[]{:S(2)}, u32[]{:S(2)}) %all-to-all-start) | async-done | bytes 1311264 | tf_op jit(solution)/shard_map/while/body/eval_jaxpr/all_to_all | solution.py:11
  644.5 2.9 fusion.71
  652.6 3.7 all-to-all-start
  660.7 17.7 %all-to-all-done = f32[16,1,20488]{2,1,0:T(1,128)S(1)} async-done(((f32[16,1,20488]{2,1,0:T(1,128)}), f32[16,1,20488]{2,1,0:T(1,128)S(1)}, u32[]{:S(2)}, u32[]{:S(2)}) %all-to-all-start) | async-done | bytes 1311264 | tf_op jit(solution)/shard_map/while/body/eval_jaxpr/all_to_all | solution.py:11
  (551 shorter events, 266.3 us)
Async XLA Ops:
  3.8 6.1 copy-start.2
  9.9 9.5 %copy-start.6 = (f32[1,5]{1,0:T(1,128)S(1)}, f32[1,5]{1,0:T(1,128)}, u32[]{:S(2)}) copy-start(f32[1,5]{1,0:T(1,128)} %param.25) | copy-start | bytes 64
  9.9 10.1 %copy-start.4 = (f32[1,5,64]{2,0,1:T(1,128)S(1)}, f32[1,5,64]{2,0,1:T(1,128)}, u32[]{:S(2)}) copy-start(f32[1,5,64]{2,0,1:T(1,128)} %param.28) | copy-start | bytes 3844
  10.0 10.1 %copy-start.5 = (f32[1,5,64]{2,0,1:T(1,128)S(1)}, f32[1,5,64]{2,0,1:T(1,128)}, u32[]{:S(2)}) copy-start(f32[1,5,64]{2,0,1:T(1,128)} %param.31) | copy-start | bytes 3844
  10.0 10.6 %copy-start.3 = (f32[1,4,5,64]{3,1,2,0:T(4,128)S(1)}, f32[1,4,5,64]{3,1,2,0:T(4,128)}, u32[]{:S(2)}) copy-start(f32[1,4,5,64]{3,1,2,0:T(4,128)} %param.27) | copy-start | bytes 15364
  10.8 19.0 %all-to-all-start.1 = ((bf16[16,64,160]{2,1,0:T(8,128)(2,1)}), bf16[16,64,160]{2,1,0:T(8,128)(2,1)S(1)}, u32[]{:S(2)}, u32[]{:S(2)}) async-start(bf16[16,64,160]{2,1,0:T(8,128)(2,1)} %broadcast_in_dim.100), calls=%async_computation.1 | async-start | bytes 1048576 | tf_op jit(solution)/shard_map/all_to_all | solution.py:11
  26.2 5.3 copy-start
  26.2 5.3 copy-start.1
  45.4 21.5 %all-to-all-start = ((f32[16,1,20488]{2,1,0:T(1,128)}), f32[16,1,20488]{2,1,0:T(1,128)S(1)}, u32[]{:S(2)}, u32[]{:S(2)}) async-start(f32[16,1,20488]{2,1,0:T(1,128)} %broadcast_in_dim.102), calls=%async_computation | async-start | bytes 2637824 | tf_op jit(solution)/shard_map/while/body/eval_jaxpr/all_to_all | solution.py:11
  67.9 7.8 %collective-permute-start = (bf16[8,2560]{1,0:T(8,128)(2,1)S(1)}, bf16[8,2560]{1,0:T(8,128)(2,1)S(1)}, u32[]{:S(2)}, u32[]{:S(2)}) collective-permute-start(bf16[8,2560]{1,0:T(8,128)(2,1)S(1)} %fusion.78), channel_id=1, source_target_pairs={{0,16},{16,32},{32,48},{48,64},{64,80},{80,96},{96,112},{1,17},{17... | collective-permute-start | bytes 122888 | tf_op jit(solution)/shard_map/while/body/eval_jaxpr/ppermute | solution.py:42
  89.5 23.4 %all-to-all-start = ((f32[16,1,20488]{2,1,0:T(1,128)}), f32[16,1,20488]{2,1,0:T(1,128)S(1)}, u32[]{:S(2)}, u32[]{:S(2)}) async-start(f32[16,1,20488]{2,1,0:T(1,128)} %broadcast_in_dim.102), calls=%async_computation | async-start | bytes 2637824 | tf_op jit(solution)/shard_map/while/body/eval_jaxpr/all_to_all | solution.py:11
  113.9 6.2 collective-permute-start
  133.9 22.1 %all-to-all-start = ((f32[16,1,20488]{2,1,0:T(1,128)}), f32[16,1,20488]{2,1,0:T(1,128)S(1)}, u32[]{:S(2)}, u32[]{:S(2)}) async-start(f32[16,1,20488]{2,1,0:T(1,128)} %broadcast_in_dim.102), calls=%async_computation | async-start | bytes 2637824 | tf_op jit(solution)/shard_map/while/body/eval_jaxpr/all_to_all | solution.py:11
  157.0 7.1 %collective-permute-start = (bf16[8,2560]{1,0:T(8,128)(2,1)S(1)}, bf16[8,2560]{1,0:T(8,128)(2,1)S(1)}, u32[]{:S(2)}, u32[]{:S(2)}) collective-permute-start(bf16[8,2560]{1,0:T(8,128)(2,1)S(1)} %fusion.78), channel_id=1, source_target_pairs={{0,16},{16,32},{32,48},{48,64},{64,80},{80,96},{96,112},{1,17},{17... | collective-permute-start | bytes 122888 | tf_op jit(solution)/shard_map/while/body/eval_jaxpr/ppermute | solution.py:42
  177.9 21.4 %all-to-all-start = ((f32[16,1,20488]{2,1,0:T(1,128)}), f32[16,1,20488]{2,1,0:T(1,128)S(1)}, u32[]{:S(2)}, u32[]{:S(2)}) async-start(f32[16,1,20488]{2,1,0:T(1,128)} %broadcast_in_dim.102), calls=%async_computation | async-start | bytes 2637824 | tf_op jit(solution)/shard_map/while/body/eval_jaxpr/all_to_all | solution.py:11
  200.3 6.6 collective-permute-start
  220.7 21.7 %all-to-all-start = ((f32[16,1,20488]{2,1,0:T(1,128)}), f32[16,1,20488]{2,1,0:T(1,128)S(1)}, u32[]{:S(2)}, u32[]{:S(2)}) async-start(f32[16,1,20488]{2,1,0:T(1,128)} %broadcast_in_dim.102), calls=%async_computation | async-start | bytes 2637824 | tf_op jit(solution)/shard_map/while/body/eval_jaxpr/all_to_all | solution.py:11
  243.4 6.3 collective-permute-start
  263.6 21.9 %all-to-all-start = ((f32[16,1,20488]{2,1,0:T(1,128)}), f32[16,1,20488]{2,1,0:T(1,128)S(1)}, u32[]{:S(2)}, u32[]{:S(2)}) async-start(f32[16,1,20488]{2,1,0:T(1,128)} %broadcast_in_dim.102), calls=%async_computation | async-start | bytes 2637824 | tf_op jit(solution)/shard_map/while/body/eval_jaxpr/all_to_all | solution.py:11
  286.4 6.0 collective-permute-start
  306.4 22.3 %all-to-all-start = ((f32[16,1,20488]{2,1,0:T(1,128)}), f32[16,1,20488]{2,1,0:T(1,128)S(1)}, u32[]{:S(2)}, u32[]{:S(2)}) async-start(f32[16,1,20488]{2,1,0:T(1,128)} %broadcast_in_dim.102), calls=%async_computation | async-start | bytes 2637824 | tf_op jit(solution)/shard_map/while/body/eval_jaxpr/all_to_all | solution.py:11
  329.6 5.7 collective-permute-start
  349.2 22.8 %all-to-all-start = ((f32[16,1,20488]{2,1,0:T(1,128)}), f32[16,1,20488]{2,1,0:T(1,128)S(1)}, u32[]{:S(2)}, u32[]{:S(2)}) async-start(f32[16,1,20488]{2,1,0:T(1,128)} %broadcast_in_dim.102), calls=%async_computation | async-start | bytes 2637824 | tf_op jit(solution)/shard_map/while/body/eval_jaxpr/all_to_all | solution.py:11
  372.9 5.2 collective-permute-start
  392.0 23.5 %all-to-all-start = ((f32[16,1,20488]{2,1,0:T(1,128)}), f32[16,1,20488]{2,1,0:T(1,128)S(1)}, u32[]{:S(2)}, u32[]{:S(2)}) async-start(f32[16,1,20488]{2,1,0:T(1,128)} %broadcast_in_dim.102), calls=%async_computation | async-start | bytes 2637824 | tf_op jit(solution)/shard_map/while/body/eval_jaxpr/all_to_all | solution.py:11
  416.4 4.5 collective-permute-start
  434.8 25.1 %all-to-all-start = ((f32[16,1,20488]{2,1,0:T(1,128)}), f32[16,1,20488]{2,1,0:T(1,128)S(1)}, u32[]{:S(2)}, u32[]{:S(2)}) async-start(f32[16,1,20488]{2,1,0:T(1,128)} %broadcast_in_dim.102), calls=%async_computation | async-start | bytes 2637824 | tf_op jit(solution)/shard_map/while/body/eval_jaxpr/all_to_all | solution.py:11
  460.8 3.1 collective-permute-start
  477.8 25.8 %all-to-all-start = ((f32[16,1,20488]{2,1,0:T(1,128)}), f32[16,1,20488]{2,1,0:T(1,128)S(1)}, u32[]{:S(2)}, u32[]{:S(2)}) async-start(f32[16,1,20488]{2,1,0:T(1,128)} %broadcast_in_dim.102), calls=%async_computation | async-start | bytes 2637824 | tf_op jit(solution)/shard_map/while/body/eval_jaxpr/all_to_all | solution.py:11
  504.5 3.1 collective-permute-start
  521.5 25.8 %all-to-all-start = ((f32[16,1,20488]{2,1,0:T(1,128)}), f32[16,1,20488]{2,1,0:T(1,128)S(1)}, u32[]{:S(2)}, u32[]{:S(2)}) async-start(f32[16,1,20488]{2,1,0:T(1,128)} %broadcast_in_dim.102), calls=%async_computation | async-start | bytes 2637824 | tf_op jit(solution)/shard_map/while/body/eval_jaxpr/all_to_all | solution.py:11
  548.3 3.1 collective-permute-start
  565.2 25.8 %all-to-all-start = ((f32[16,1,20488]{2,1,0:T(1,128)}), f32[16,1,20488]{2,1,0:T(1,128)S(1)}, u32[]{:S(2)}, u32[]{:S(2)}) async-start(f32[16,1,20488]{2,1,0:T(1,128)} %broadcast_in_dim.102), calls=%async_computation | async-start | bytes 2637824 | tf_op jit(solution)/shard_map/while/body/eval_jaxpr/all_to_all | solution.py:11
  592.0 3.1 collective-permute-start
  608.9 25.8 %all-to-all-start = ((f32[16,1,20488]{2,1,0:T(1,128)}), f32[16,1,20488]{2,1,0:T(1,128)S(1)}, u32[]{:S(2)}, u32[]{:S(2)}) async-start(f32[16,1,20488]{2,1,0:T(1,128)} %broadcast_in_dim.102), calls=%async_computation | async-start | bytes 2637824 | tf_op jit(solution)/shard_map/while/body/eval_jaxpr/all_to_all | solution.py:11
  635.7 3.1 collective-permute-start
  652.6 25.8 %all-to-all-start = ((f32[16,1,20488]{2,1,0:T(1,128)}), f32[16,1,20488]{2,1,0:T(1,128)S(1)}, u32[]{:S(2)}, u32[]{:S(2)}) async-start(f32[16,1,20488]{2,1,0:T(1,128)} %broadcast_in_dim.102), calls=%async_computation | async-start | bytes 2637824 | tf_op jit(solution)/shard_map/while/body/eval_jaxpr/all_to_all | solution.py:11
  679.4 3.1 collective-permute-start
where the time goes:
time: 691 us; the launch traced here: 682 us
  waiting for transfers between devices  244 us (35%)
  other arithmetic  146 us (21%)
  starting transfers between devices  121 us (18%)
  matrix products  87.4 us (13%)
  local copies, waits for them, and re-layouts  81.9 us (12%)
    all_to_all x16, waiting for transfers between devices, copy_for_each(): lax.all_to_all(jnp.broadcast_to(array[None], (size, *array.shape)), axis,...  237 us
    dynamic_update_slice x60, other arithmetic, put_rows(): return lax.dynamic_update_slice(buffer, chosen[None], tuple(corner))  64.7 us
    all_to_all x16, starting transfers between devices, copy_for_each(): lax.all_to_all(jnp.broadcast_to(array[None], (size, *array.shape)), axis,...  64.1 us
    ppermute x15, starting transfers between devices, shifted(): lax.ppermute(value, axis, [(source, source + steps) for source in range(l...  57 us
    dot_general x15, matrix products, mixer_core(): jnp.dot(normed, w_zx.reshape(model_width, head_count * 2 * head_size), pr...  43.2 us
    reduce_sum x15, other arithmetic, mixer_core(): jnp.sum(state_f * c_output[:, None, None, :], axis=-1)  29 us
    broadcast_in_dim x16, local copies, waits for them, and re-layouts, copy_for_each(): jnp.broadcast_to(array[None], (size, *array.shape))  27.2 us
    dot_general x15, matrix products, mixer_core(): jnp.dot(normed, w_bc, preferred_element_type=jnp.float32)  24.5 us
  transfers between devices with their start and end apart: 31, of which 31 were waited for; matrix products, arithmetic and copies ran while one was open for 12% of the time, Pallas kernels for 0%

commit v1 on v0

v1 whole, which is shorter than its diff:
```python
import functools

import jax
import jax.numpy as jnp
from jax import lax
from jax.experimental import pallas as pl
from jax.experimental.pallas import tpu as pltpu
from jax.sharding import PartitionSpec as P

epsilon = 1e-05
MESH = pl.DeviceIdType.MESH
F32, BF16 = jnp.float32, jnp.bfloat16
SIDE = 4
NEAR = (0, 1, 3, 2)
FAR = (2, 1, 3, 0)


def silu(v):
    return v / (1.0 + jnp.exp(-v))


def softplus(v):
    return jnp.maximum(v, 0.0) + jnp.log1p(jnp.exp(-jnp.abs(v)))


def kernel(
    sections,
    hid_ref,
    gain_ref,
    wzx_hbm,
    wbc_hbm,
    wdt_ref,
    dtb_ref,
    alog_ref,
    dsk_ref,
    cxw_ref,
    cxb_ref,
    cbw_ref,
    cbb_ref,
    ig_ref,
    wout_hbm,
    cxs_ref,
    cbs_ref,
    ssm_hbm,
    sec_out,
    cx_out,
    cb_out,
    ssm_out,
    w_all,
    w_o,
    st,
    hbuf,
    acc,
    wdt_pad,
    pre_bc,
    pre_x,
    par,
    q_buf,
    inner,
    stx,
    dec,
    b_buf,
    xf_buf,
    stx_t,
    dec_t,
    send_buf,
    rs_buf,
    ag_src,
    init_buf,
    sh_buf,
    load_sem,
    out_sem,
    init_send,
    init_recv,
    rs_send,
    rs_recv,
    ag_send,
    ag_recv,
    sh_send,
    sh_recv,
):
    heads, streams, p_size = cxs_ref.shape[1:]
    width, n2 = wbc_hbm.shape
    n_state = n2 // 2
    chunk = width // SIDE
    rows = streams // SIDE
    share = hid_ref.shape[1]
    team = SIDE * SIDE
    last = sections - 1

    sec = lax.axis_index("section")
    me = lax.axis_index("tensor")
    my_z = me // SIDE
    my_y = me % SIDE

    def dev(s, t):
        return {"section": s, "tensor": t}

    loads = [pltpu.make_async_copy(wbc_hbm, w_all.at[:, pl.ds(0, n2)], load_sem.at[0])]
    for h in range(heads):
        loads.append(
            pltpu.make_async_copy(
                wzx_hbm.at[h], w_all.at[:, pl.ds(n2 + 128 * h, 128)], load_sem.at[1 + h]
            )
        )
    at = 1 + heads
    for yy in range(SIDE):
        loads.append(
            pltpu.make_async_copy(
                wout_hbm.at[:, pl.ds(chunk * yy, chunk)], w_o.at[yy], load_sem.at[at + yy]
            )
        )
    at += SIDE
    loads.append(pltpu.make_async_copy(ssm_hbm, st, load_sem.at[at]))

    barrier = pltpu.get_barrier_semaphore()

    def greet(j, carry):
        other = (me + j) % team

        @pl.when(j > 0)
        def _():
            pl.semaphore_signal(barrier, inc=1, device_id=dev(sec, other), device_id_type=MESH)

        @pl.when(sec > 0)
        def _():
            pl.semaphore_signal(barrier, inc=1, device_id=dev(sec - 1, other), device_id_type=MESH)

        @pl.when(sec < last)
        def _():
            pl.semaphore_signal(barrier, inc=1, device_id=dev(sec + 1, other), device_id_type=MESH)

        return carry

    lax.fori_loop(0, team, greet, 0)
    for cp in loads:
        cp.start()
    partners = team - 1 + jnp.where(sec > 0, team, 0) + jnp.where(sec < last, team, 0)
    pl.semaphore_wait(barrier, partners)

    def init_copy(dest):
        return pltpu.make_async_remote_copy(
            src_ref=hid_ref,
            dst_ref=init_buf.at[me],
            send_sem=init_send.at[dest],
            recv_sem=init_recv.at[me],
            device_id=dev(sec, dest),
            device_id_type=MESH,
        )

    def init_own():
        return pltpu.make_async_copy(hid_ref, init_buf.at[me], init_recv.at[me])

    @pl.when(sec == 0)
    def _():
        def go(j, carry):
            init_copy((me + j) % team).start()
            return carry

        lax.fori_loop(1, team, go, 0)
        init_own().start()

    lane = lax.broadcasted_iota(jnp.int32, (streams, 128), 1)
    low = lane < p_size
    wdt_pad[...] = jnp.zeros_like(wdt_pad)
    wdt_pad[0:heads, :] = wdt_ref[...].astype(F32)
    for h in range(1 + heads):
        loads[h].wait()
    for j in range(width // 128):
        blk = wdt_pad[:, 128 * j : 128 * j + 128]
        w_all[128 * j : 128 * j + 128, n2 + 128 * heads : n2 + 128 * heads + 128] = blk.T.astype(BF16)
    acc[...] = jnp.zeros_like(acc)
    q_buf[...] = jnp.zeros_like(q_buf)
    cbw = cbw_ref[...]
    pre_bc[...] = (
        cbs_ref[0].astype(F32) * cbw[0:1]
        + cbs_ref[1].astype(F32) * cbw[1:2]
        + cbs_ref[2].astype(F32) * cbw[2:3]
        + cbb_ref[...]
    )
    pairs = (heads + 1) // 2

    def packed(get, k):
        a = get(2 * k)
        b = get(2 * k + 1) if 2 * k + 1 < heads else jnp.zeros_like(a)
        return jnp.concatenate([a, b], axis=1)

    def pre_of(h):
        w = cxw_ref[h]
        return (
            cxs_ref[0, h].astype(F32) * w[0:1]
            + cxs_ref[1, h].astype(F32) * w[1:2]
            + cxs_ref[2, h].astype(F32) * w[2:3]
            + cxb_ref[h]
        )

    for k in range(pairs):
        pre_x[k] = packed(pre_of, k)
        par[0, k] = packed(lambda h: cxw_ref[h][3:4], k)
        par[1, k] = packed(lambda h: ig_ref[h], k)
        par[2, k] = packed(
            lambda h: jnp.broadcast_to(dsk_ref[:, h : h + 1], (1, p_size)), k
        )
    pad = jnp.zeros((1, 128 - heads), F32)
    dtb = jnp.concatenate([dtb_ref[...], pad], axis=1)
    neg_a = -jnp.exp(jnp.concatenate([alog_ref[...], pad], axis=1))

    @pl.when(sec == 0)
    def _():
        def wait_one(k, carry):
            pltpu.make_async_copy(hid_ref, init_buf.at[k], init_recv.at[k]).wait()
            return carry

        lax.fori_loop(0, team, wait_one, 0)
        for yy in range(SIDE):
            parts = [init_buf[SIDE * yy + i].astype(F32) for i in range(SIDE)]
            hbuf[yy] = jnp.concatenate(parts, axis=1).astype(BF16)

    def ag_copy(src_t, dest):
        return pltpu.make_async_remote_copy(
            src_ref=ag_src,
            dst_ref=hbuf.at[src_t % SIDE, pl.ds(pl.multiple_of((src_t // SIDE) * rows, rows), rows), :],
            send_sem=ag_send.at[dest],
            recv_sem=ag_recv.at[src_t],
            device_id=dev(jnp.minimum(sec + 1, last), dest),
            device_id_type=MESH,
        )

    sq = jnp.zeros((streams, 128), F32)
    for off in NEAR:
        yy = (my_y + off) % SIDE

        @pl.when(sec > 0)
        def _():
            for zo in NEAR:
                ag_copy(((my_z + zo) % SIDE) * SIDE + yy, me).wait_recv()

        hv = hbuf[yy].astype(F32)
        for i in range(chunk // 128):
            part = hv[:, 128 * i : 128 * i + 128]
            sq = sq + part * part
        start = pl.multiple_of(yy * chunk, chunk)
        hg = (hv * gain_ref[:, pl.ds(start, chunk)]).astype(BF16)
        acc[...] += jnp.dot(hg, w_all[pl.ds(start, chunk), :], preferred_element_type=F32)
    r = lax.rsqrt(jnp.sum(sq, axis=1, keepdims=True) * (1.0 / width) + epsilon)

    bcf = (acc[:, 0:n2] * r).astype(BF16)
    cb_out[0] = cbs_ref[1]
    cb_out[1] = cbs_ref[2]
    cb_out[2] = bcf
    bcv = silu(pre_bc[...] + bcf.astype(F32) * cbw[3:4])
    b_in = bcv[:, 0:n_state]
    c_out = bcv[:, n_state:n2]
    b_buf[...] = b_in
    bd = jnp.sum(b_in * c_out, axis=1, keepdims=True)
    c_bf = c_out

    loads[-1].wait()
    group = 16
    row = lax.broadcasted_iota(jnp.int32, (group, n_state), 0)
    for g in range(streams // group):
        c16 = c_bf[group * g : group * g + group]
        total = None
        for i in range(0, group, 2):
            lhs = jnp.concatenate(
                [jnp.where(row == i, c16, 0.0), jnp.where(row == i + 1, c16, 0.0)], axis=1
            ).astype(BF16)
            rhs = jnp.concatenate([st[group * g + i], st[group * g + i + 1]], axis=1)
            term = lax.dot_general(
                lhs, rhs, (((1,), (1,)), ((), ())), preferred_element_type=F32
            )
            total = term if total is None else total + term
        q_buf[group * g : group * g + group, 0 : heads * p_size] = total

    dt0 = n2 + 128 * heads
    step = softplus(acc[:, dt0 : dt0 + 128] * r + dtb)
    decay = jnp.exp(step * neg_a)

    def spread(v, k):
        hi = min(2 * k + 1, heads - 1)
        a = jnp.broadcast_to(v[:, 2 * k : 2 * k + 1], (streams, 128))
        b = jnp.broadcast_to(v[:, hi : hi + 1], (streams, 128))
        return jnp.where(low, a, b)

    sq = jnp.zeros((streams, 128), F32)
    for k in range(pairs):
        a = acc[:, n2 + 256 * k : n2 + 256 * k + 128]
        if 2 * k + 1 < heads:
            b = acc[:, n2 + 256 * k + 128 : n2 + 256 * k + 256]
        else:
            b = jnp.zeros_like(a)
        x_new = jnp.where(low, pltpu.roll(a, p_size, 1), b)
        z_new = jnp.where(low, a, pltpu.roll(b, p_size, 1))
        xf = (x_new * r).astype(BF16)
        xf_buf[k] = xf
        xc = silu(pre_x[k] + xf.astype(F32) * par[0, k])
        sk = spread(step, k)
        dk = spread(decay, k)
        sx = sk * xc
        stx[k] = sx
        dec[k] = dk
        q = q_buf[:, 128 * k : 128 * k + 128]
        y_out = dk * q + sx * bd + par[2, k] * xc
        gated = y_out * silu(z_new * r)
        sq = sq + gated * gated
        inner[:, 128 * k : 128 * k + 128] = (gated * par[1, k]).astype(BF16)
    squares = jnp.sum(sq, axis=1, keepdims=True)
    hi = squares.astype(BF16).astype(F32)
    lo = squares - hi
    sq_tile = jnp.where(lane == 0, hi, jnp.where(lane == 1, lo, 0.0)).astype(BF16)

    def rs_copy(src_t, dest, yy, zz):
        return pltpu.make_async_remote_copy(
            src_ref=send_buf.at[yy, pl.ds(pl.multiple_of(zz * rows, rows), rows), :],
            dst_ref=rs_buf.at[src_t],
            send_sem=rs_send.at[dest],
            recv_sem=rs_recv.at[src_t],
            device_id=dev(sec, dest),
            device_id_type=MESH,
        )

    for yo in FAR:
        yy = (my_y + yo) % SIDE
        if yo == FAR[0]:
            for cp in loads[1 + heads : 1 + heads + SIDE]:
                cp.wait()
        part = jnp.dot(
            inner[:, 0 : heads * p_size], w_o[yy], preferred_element_type=F32
        )
        send_buf[yy, :, 0:chunk] = part.astype(BF16)
        send_buf[yy, :, chunk : chunk + 128] = sq_tile
        for zo in FAR:
            zz = (my_z + zo) % SIDE
            dest = zz * SIDE + yy
            if yo == 0 and zo == 0:
                pltpu.make_async_copy(
                    send_buf.at[yy, pl.ds(pl.multiple_of(zz * rows, rows), rows), :],
                    rs_buf.at[me],
                    rs_recv.at[me],
                ).start()
            else:
                rs_copy(me, dest, yy, zz).start()

    tot = jnp.zeros((rows, chunk + 128), F32)
    for yo in NEAR:
        for zo in NEAR:
            src = ((my_z + zo) % SIDE) * SIDE + (my_y + yo) % SIDE
            if yo == 0 and zo == 0:
                pltpu.make_async_copy(
                    send_buf.at[0, pl.ds(0, rows), :], rs_buf.at[src], rs_recv.at[src]
                ).wait()
            else:
                rs_copy(src, me, my_y, my_z).wait_recv()
            tot = tot + rs_buf[src].astype(F32)
    scale = lax.rsqrt(
        jnp.sum(tot[:, chunk : chunk + 128], axis=1, keepdims=True)
        * (1.0 / (heads * p_size * team))
        + epsilon
    )
    mine = hbuf[my_y, pl.ds(pl.multiple_of(my_z * rows, rows), rows), :].astype(F32)
    ag_src[...] = (mine + tot[:, 0:chunk] * scale).astype(BF16)

    @pl.when(sec < last)
    def _():
        for yo in FAR:
            for zo in FAR:
                ag_copy(me, ((my_z + zo) % SIDE) * SIDE + (my_y + yo) % SIDE).start()

    def sh_copy(src_z, j):
        return pltpu.make_async_remote_copy(
            src_ref=ag_src,
            dst_ref=sh_buf.at[src_z],
            send_sem=sh_send.at[j],
            recv_sem=sh_recv.at[src_z],
            device_id=dev(sec, my_y * SIDE + j),
            device_id_type=MESH,
        )

    def sh_own():
        return pltpu.make_async_copy(ag_src, sh_buf.at[my_z], sh_recv.at[my_z])

    for j in range(SIDE):
        own = my_y * SIDE + j == me

        @pl.when(own)
        def _():
            sh_own().start()

        @pl.when(jnp.logical_not(own))
        def _():
            sh_copy(my_z, j).start()

    zeros = jnp.zeros((128 - streams, 128), F32)
    for k in range(pairs):
        stx_t[128 * k : 128 * k + 128] = jnp.concatenate([stx[k], zeros], axis=0).T
        dec_t[128 * k : 128 * k + 128] = jnp.concatenate([dec[k], zeros], axis=0).T
    hp = heads * p_size
    octet = 8

    def out_copy(g):
        span = pl.ds(pl.multiple_of(g * octet, octet), octet)
        return pltpu.make_async_copy(st.at[span], ssm_out.at[span], out_sem.at[g])

    def update(g, carry):
        shift = (128 - g * octet) % 128
        b8 = b_buf[pl.ds(pl.multiple_of(g * octet, octet), octet), :]
        for half in range(heads):
            span = slice(p_size * half, p_size * half + p_size)
            sx_r = pltpu.roll(stx_t[span, :], shift, 1)
            dk_r = pltpu.roll(dec_t[span, :], shift, 1)
            for i in range(octet):
                old = st[g * octet + i, span, :].astype(F32)
                new = (
                    jnp.broadcast_to(dk_r[:, i : i + 1], (p_size, 128)) * old
                    + jnp.broadcast_to(sx_r[:, i : i + 1], (p_size, 128)) * b8[i : i + 1]
                )
                st[g * octet + i, span, :] = new.astype(BF16)
        out_copy(g).start()
        return carry

    lax.fori_loop(0, streams // octet, update, 0)

    cx_out[0] = cxs_ref[1]
    cx_out[1] = cxs_ref[2]
    for h in range(heads):
        xf = xf_buf[h // 2].astype(F32)
        cx_out[2, h] = xf[:, p_size * (h % 2) : p_size * (h % 2) + p_size].astype(BF16)

    for zz in range(SIDE):
        sh_copy(zz, 0).wait_recv()
    for yy in range(SIDE):

        @pl.when(my_y == yy)
        def _():
            for zz in range(SIDE):
                sec_out[rows * zz : rows * zz + rows, :] = (
                    sh_buf[zz].astype(F32)[:, share * yy : share * yy + share].astype(BF16)
                )

    for yo in FAR:
        for zo in FAR:
            dest = ((my_z + zo) % SIDE) * SIDE + (my_y + yo) % SIDE
            if not (yo == 0 and zo == 0):
                rs_copy(me, dest, my_y, my_z).wait_send()

    @pl.when(sec < last)
    def _():
        for dest in range(team):
            ag_copy(me, dest).wait_send()

    for j in range(SIDE):

        @pl.when(my_y * SIDE + j != me)
        def _():
            sh_copy(my_z, j).wait_send()

    @pl.when(sec == 0)
    def _():
        def sent(j, carry):
            init_copy((me + j) % team).wait_send()
            return carry

        lax.fori_loop(1, team, sent, 0)

    def written(g, carry):
        out_copy(g).wait()
        return carry

    lax.fori_loop(0, streams // octet, written, 0)


def shards(
    hidden_in,
    pre_gain,
    w_zx,
    w_bc,
    w_dt,
    dt_bias,
    a_log,
    d_skip,
    conv_x_weight,
    conv_x_bias,
    conv_bc_weight,
    conv_bc_bias,
    inner_gain,
    w_out,
    conv_x_state,
    conv_bc_state,
    ssm_state,
    sections,
):
    streams, share = hidden_in.shape
    _, heads, p_size, width = w_out.shape
    n2 = w_bc.shape[2]
    n_state = n2 // 2
    team = SIDE * SIDE
    chunk, rows = width // SIDE, streams // SIDE
    hp = heads * p_size
    cols = n2 + 128 * heads + 128
    pairs = (heads + 1) // 2
    args = (
        hidden_in,
        pre_gain,
        jnp.transpose(w_zx[0], (1, 0, 2)),
        w_bc[0],
        jnp.transpose(w_dt[0], (1, 0)),
        dt_bias,
        a_log,
        d_skip,
        jnp.transpose(conv_x_weight[0], (1, 0, 2)),
        jnp.transpose(conv_x_bias, (1, 0, 2)),
        conv_bc_weight[0],
        conv_bc_bias,
        jnp.transpose(inner_gain, (1, 0, 2)),
        w_out[0].reshape(hp, width),
        jnp.transpose(conv_x_state[0], (1, 2, 0, 3)),
        jnp.transpose(conv_bc_state[0], (1, 0, 2)),
        ssm_state[0].reshape(streams, hp, n_state),
    )
    vmem = pl.BlockSpec(memory_space=pltpu.VMEM)
    hbm = pl.BlockSpec(memory_space=pl.ANY)
    large = (2, 3, 13, 16)
    dma = pltpu.SemaphoreType.DMA
    sec_new, cx_new, cb_new, ssm_new = pl.pallas_call(
        functools.partial(kernel, sections),
        out_shape=(
            jax.ShapeDtypeStruct((streams, share), BF16),
            jax.ShapeDtypeStruct((3, heads, streams, p_size), BF16),
            jax.ShapeDtypeStruct((3, streams, n2), BF16),
            jax.ShapeDtypeStruct((streams, hp, n_state), BF16),
        ),
        in_specs=[hbm if i in large else vmem for i in range(len(args))],
        out_specs=(vmem, vmem, vmem, hbm),
        scratch_shapes=[
            pltpu.VMEM((width, cols), BF16),
            pltpu.VMEM((SIDE, hp, chunk), BF16),
            pltpu.VMEM((streams, hp, n_state), BF16),
            pltpu.VMEM((SIDE, streams, chunk), BF16),
            pltpu.VMEM((streams, cols), F32),
            pltpu.VMEM((128, width), F32),
            pltpu.VMEM((streams, n2), F32),
            pltpu.VMEM((pairs, streams, 128), F32),
            pltpu.VMEM((3, pairs, 1, 128), F32),
            pltpu.VMEM((streams, 128 * pairs), F32),
            pltpu.VMEM((streams, 128 * pairs), BF16),
            pltpu.VMEM((pairs, streams, 128), F32),
            pltpu.VMEM((pairs, streams, 128), F32),
            pltpu.VMEM((streams, n_state), F32),
            pltpu.VMEM((pairs, streams, 128), BF16),
            pltpu.VMEM((128 * pairs, 128), F32),
            pltpu.VMEM((128 * pairs, 128), F32),
            pltpu.VMEM((SIDE, streams, chunk + 128), BF16),
            pltpu.VMEM((team, rows, chunk + 128), BF16),
            pltpu.VMEM((rows, chunk), BF16),
            pltpu.VMEM((team, streams, share), BF16),
            pltpu.VMEM((SIDE, rows, chunk), BF16),
            dma((1 + heads + SIDE + 1,)),
            dma((8,)),
            dma((team,)),
            dma((team,)),
            dma((team,)),
            dma((team,)),
            dma((team,)),
            dma((team,)),
            dma((SIDE,)),
            dma((SIDE,)),
        ],
        compiler_params=pltpu.CompilerParams(
            collective_id=0, has_side_effects=True, vmem_limit_bytes=40 * 1024 * 1024
        ),
        name="stack_step",
    )(*args)
    return (
        sec_new[None],
        jnp.transpose(cx_new, (2, 0, 1, 3))[None],
        jnp.transpose(cb_new, (1, 0, 2))[None],
        ssm_new.reshape(ssm_state.shape),
    )


def solution(mesh):
    placed = (
        P(None, "tensor"),
        P("section", None),
        P("section", None, "tensor", None),
        P("section", None, None),
        P("section", None, "tensor"),
        P("section", "tensor"),
        P("section", "tensor"),
        P("section", "tensor"),
        P("section", None, "tensor", None),
        P("section", "tensor", None),
        P("section", None, None),
        P("section", None),
        P("section", "tensor", None),
        P("section", "tensor", None, None),
        P("section", None, None, "tensor", None),
        P("section", None, None, None),
        P("section", None, "tensor", None, None),
    )
    return jax.shard_map(
        functools.partial(shards, sections=mesh.shape["section"]),
        mesh=mesh,
        in_specs=placed,
        out_specs=(
            P("section", None, "tensor"),
            P("section", None, None, "tensor", None),
            P("section", None, None, None),
            P("section", None, "tensor", None, None),
        ),
        check_vma=False,
    )
```

time: 691 us -> 159 us (0.23)
  the two profiles are of different devices: /device:TPU:1 before, /device:TPU:7 now
where the time goes in v1:
time: 159 us; the launch traced here: 158 us
  Pallas kernels  139 us (87%)
  local copies, waits for them, and re-layouts  18.4 us (12%)
    pallas_call x1, Pallas kernels, shards(): pl.pallas_call(functools.partial(kernel, sections), out_shape=(jax.ShapeD...  139 us
    unnamed x36, local copies, waits for them, and re-layouts  18.4 us

profile of v1, /device:TPU:7, one launch (start us, length us, event | category | flops | bytes accessed | tf_op | source)
XLA Modules:
  0.0 158.1 jit_solution(8035431262900495754)
XLA Ops:
  0.6 0.0 copy-start
  0.6 1.9 %copy-done = bf16[1,2560,5,128]{3,1,2,0:T(8,128)(2,1)S(1)} copy-done((bf16[1,2560,5,128]{3,1,2,0:T(8,128)(2,1)S(1)}, bf16[1,2560,5,128]{3,1,2,0:T(8,128)(2,1)}, u32[]{:S(2)}) %copy-start) | copy-done | bytes 3276824
  2.6 0.0 copy-start.1
  2.6 1.4 copy-done.1
  4.0 0.0 copy-start.2
  4.0 1.3 copy-done.2
  5.3 0.0 copy-start.3
  5.3 0.9 copy-done.3
  6.3 0.0 copy-start.4
  6.3 0.9 copy-done.4
  7.2 0.0 copy-start.5
  7.2 0.8 copy-done.5
  7.9 0.0 copy-start.6
  7.9 0.8 copy-done.6
  8.7 0.0 copy-start.7
  8.7 0.7 copy-done.7
  9.4 0.0 copy-start.8
  9.4 0.7 copy-done.8
  10.1 0.0 copy-start.9
  10.1 0.7 copy-done.9
  10.8 0.0 copy-start.10
  10.8 0.7 copy-done.10
  11.5 0.0 copy-start.11
  11.5 0.7 copy-done.11
  12.1 0.0 copy-start.12
  12.2 0.7 copy-done.12
  12.8 0.0 copy-start.13
  12.8 0.7 copy-done.13
  13.5 0.0 copy-start.14
  13.5 0.7 copy-done.14
  14.1 0.0 copy-start.15
  14.1 0.7 copy-done.15
  14.8 139.0 %stack_step.1 = (bf16[64,160]{1,0:T(8,128)(2,1)S(1)}, bf16[3,5,64,64]{3,2,1,0:T(8,128)(2,1)S(1)}, bf16[3,64,256]{2,1,0:T(8,128)(2,1)S(1)}, bf16[64,320,128]{2,1,0:T(8,128)(2,1)S(1)}) custom-call(bf16[64,160]{1,0:T(8,128)(2,1)S(1)} %copy-done.6, f32[1,2560]{1,0:T(1,128)S(1)} %copy-done.7, bf16[5,2560,128]{2,1,0:T(8,128)(2,1)S(1)} %bitcast.30, ...), custom_call_target="tpu_custom_call" | custom-call | tf_op jit(solution)/shard_map/stack_step/pallas_call | solution.py:524
  153.8 0.6 copy.25
  154.4 0.7 copy.26
  155.1 0.6 copy.27
  155.8 2.4 %copy.28 = bf16[1,64,5,64,128]{4,3,2,1,0:T(8,128)(2,1)} copy(bf16[1,64,5,64,128]{4,3,2,1,0:T(8,128)(2,1)S(1)} %bitcast.29) | data formatting | bytes 10485760
Async XLA Ops:
  0.6 1.9 %copy-start = (bf16[1,2560,5,128]{3,1,2,0:T(8,128)(2,1)S(1)}, bf16[1,2560,5,128]{3,1,2,0:T(8,128)(2,1)}, u32[]{:S(2)}) copy-start(bf16[1,2560,5,128]{3,1,2,0:T(8,128)(2,1)} %param.19) | copy-start | bytes 9830404
  2.6 1.4 copy-start.1
  4.0 1.3 copy-start.2
  5.3 0.9 copy-start.3
  6.3 0.9 copy-start.4
  7.2 0.8 copy-start.5
  7.9 0.8 copy-start.6
  8.7 0.7 copy-start.7
  9.4 0.7 copy-start.8
  10.1 0.7 copy-start.9
  10.8 0.7 copy-start.10
  11.5 0.7 copy-start.11
  12.1 0.7 copy-start.12
  12.8 0.7 copy-start.13
  13.5 0.7 copy-start.14
  14.1 0.7 copy-start.15

commit v2 on v1

--- a/solution.py
+++ b/solution.py
@@ -26,9 +26,27 @@
 def kernel(
     sections,
     hid_ref,
-    gain_ref,
+    gain_hbm,
     wzx_hbm,
     wbc_hbm,
+    wdt_hbm,
+    dtb_hbm,
+    alog_hbm,
+    dsk_hbm,
+    cxw_hbm,
+    cxb_hbm,
+    cbw_hbm,
+    cbb_hbm,
+    ig_hbm,
+    wout_hbm,
+    cxs_hbm,
+    cbs_hbm,
+    ssm_hbm,
+    sec_out,
+    cx_out,
+    cb_out,
+    st,
+    gain_ref,
     wdt_ref,
     dtb_ref,
     alog_ref,
@@ -38,17 +56,10 @@
     cbw_ref,
     cbb_ref,
     ig_ref,
-    wout_hbm,
     cxs_ref,
     cbs_ref,
-    ssm_hbm,
-    sec_out,
-    cx_out,
-    cb_out,
-    ssm_out,
     w_all,
     w_o,
-    st,
     hbuf,
     acc,
     wdt_pad,
@@ -69,7 +80,7 @@
     init_buf,
     sh_buf,
     load_sem,
-    out_sem,
+    small_sem,
     init_send,
     init_recv,
     rs_send,
@@ -79,7 +90,7 @@
     sh_send,
     sh_recv,
 ):
-    heads, streams, p_size = cxs_ref.shape[1:]
+    heads, streams, p_size = cxs_hbm.shape[1:]
     width, n2 = wbc_hbm.shape
     n_state = n2 // 2
     chunk = width // SIDE
@@ -112,6 +123,25 @@
         )
     at += SIDE
     loads.append(pltpu.make_async_copy(ssm_hbm, st, load_sem.at[at]))
+    smalls = [
+        pltpu.make_async_copy(a, b, small_sem.at[i])
+        for i, (a, b) in enumerate(
+            (
+                (wdt_hbm, wdt_ref),
+                (gain_hbm, gain_ref),
+                (dtb_hbm, dtb_ref),
+                (alog_hbm, alog_ref),
+                (dsk_hbm, dsk_ref),
+                (cxw_hbm, cxw_ref),
+                (cxb_hbm, cxb_ref),
+                (cbw_hbm, cbw_ref),
+                (cbb_hbm, cbb_ref),
+                (ig_hbm, ig_ref),
+                (cxs_hbm, cxs_ref),
+                (cbs_hbm, cbs_ref),
+            )
+        )
+    ]
 
     barrier = pltpu.get_barrier_semaphore()
 
@@ -132,9 +162,9 @@
 
         return carry
 
+    for cp in smalls + loads:
+        cp.start()
     lax.fori_loop(0, team, greet, 0)
-    for cp in loads:
-        cp.start()
     partners = team - 1 + jnp.where(sec > 0, team, 0) + jnp.where(sec < last, team, 0)
     pl.semaphore_wait(barrier, partners)
 
@@ -162,6 +192,8 @@
 
     lane = lax.broadcasted_iota(jnp.int32, (streams, 128), 1)
     low = lane < p_size
+    for cp in smalls:
+        cp.wait()
     wdt_pad[...] = jnp.zeros_like(wdt_pad)
     wdt_pad[0:heads, :] = wdt_ref[...].astype(F32)
     for h in range(1 + heads):
@@ -397,10 +429,6 @@
     hp = heads * p_size
     octet = 8
 
-    def out_copy(g):
-        span = pl.ds(pl.multiple_of(g * octet, octet), octet)
-        return pltpu.make_async_copy(st.at[span], ssm_out.at[span], out_sem.at[g])
-
     def update(g, carry):
         shift = (128 - g * octet) % 128
         b8 = b_buf[pl.ds(pl.multiple_of(g * octet, octet), octet), :]
@@ -415,7 +443,6 @@
                     + jnp.broadcast_to(sx_r[:, i : i + 1], (p_size, 128)) * b8[i : i + 1]
                 )
                 st[g * octet + i, span, :] = new.astype(BF16)
-        out_copy(g).start()
         return carry
 
     lax.fori_loop(0, streams // octet, update, 0)
@@ -461,12 +488,6 @@
             return carry
 
         lax.fori_loop(1, team, sent, 0)
-
-    def written(g, carry):
-        out_copy(g).wait()
-        return carry
-
-    lax.fori_loop(0, streams // octet, written, 0)
 
 
 def shards(
@@ -518,8 +539,8 @@
         ssm_state[0].reshape(streams, hp, n_state),
     )
     vmem = pl.BlockSpec(memory_space=pltpu.VMEM)
-    hbm = pl.BlockSpec(memory_space=pl.ANY)
-    large = (2, 3, 13, 16)
+    hbm = pl.BlockSpec(memory_space=pltpu.HBM)
+    small = (1, 4, 5, 6, 7, 8, 9, 10, 11, 12, 14, 15)
     dma = pltpu.SemaphoreType.DMA
     sec_new, cx_new, cb_new, ssm_new = pl.pallas_call(
         functools.partial(kernel, sections),
@@ -529,12 +550,12 @@
             jax.ShapeDtypeStruct((3, streams, n2), BF16),
             jax.ShapeDtypeStruct((streams, hp, n_state), BF16),
         ),
-        in_specs=[hbm if i in large else vmem for i in range(len(args))],
-        out_specs=(vmem, vmem, vmem, hbm),
-        scratch_shapes=[
+        in_specs=[hbm] * len(args),
+        out_specs=(vmem, vmem, vmem, vmem),
+        scratch_shapes=[pltpu.VMEM(args[i].shape, args[i].dtype) for i in small]
+        + [
             pltpu.VMEM((width, cols), BF16),
             pltpu.VMEM((SIDE, hp, chunk), BF16),
-            pltpu.VMEM((streams, hp, n_state), BF16),
             pltpu.VMEM((SIDE, streams, chunk), BF16),
             pltpu.VMEM((streams, cols), F32),
             pltpu.VMEM((128, width), F32),
@@ -555,7 +576,7 @@
             pltpu.VMEM((team, streams, share), BF16),
             pltpu.VMEM((SIDE, rows, chunk), BF16),
             dma((1 + heads + SIDE + 1,)),
-            dma((8,)),
+            dma((len(small),)),
             dma((team,)),
             dma((team,)),
             dma((team,)),
@@ -569,7 +590,7 @@
             collective_id=0, has_side_effects=True, vmem_limit_bytes=40 * 1024 * 1024
         ),
         name="stack_step",
-    )(*args)
+    )(*[pltpu.with_memory_space_constraint(a, pltpu.HBM) for a in args])
     return (
         sec_new[None],
         jnp.transpose(cx_new, (2, 0, 1, 3))[None],

time: 159 us -> 143 us (0.90)
  local copies, waits for them, and re-layouts: 18.4 us -> 4.31 us
    unnamed x36 -> x4, local copies, waits for them, and re-layouts: 18.4 us -> 4.31 us
where the time goes in v2:
time: 143 us
  Pallas kernels  138 us (97%)
  local copies, waits for them, and re-layouts  4.31 us (3%)
    pallas_call x1, Pallas kernels, shards(): pl.pallas_call(functools.partial(kernel, sections), out_shape=(jax.ShapeD...  138 us
    unnamed x4, local copies, waits for them, and re-layouts  4.31 us

profile of v2, /device:TPU:7, one launch (start us, length us, event | category | flops | bytes accessed | tf_op | source)
XLA Modules:
  0.0 142.7 jit_solution(11907590108852781435)
XLA Ops:
  0.6 137.8 %stack_step.1 = (bf16[64,160]{1,0:T(8,128)(2,1)S(1)}, bf16[3,5,64,64]{3,2,1,0:T(8,128)(2,1)S(1)}, bf16[3,64,256]{2,1,0:T(8,128)(2,1)S(1)}, bf16[64,320,128]{2,1,0:T(8,128)(2,1)S(1)}) custom-call(bf16[64,160]{1,0:T(8,128)(2,1)} %hid_ref.1, f32[1,2560]{1,0:T(1,128)} %gain_hbm.1, bf16[5,2560,128]{2,1,0:T(8,128)(2,1)} %bitcast.34, bf16[2560,256]{1,0:T(8,128)(2,1)} %bitcast.36, ...), custom_call_target="tpu_custom_call" | custom-call | tf_op jit(solution)/shard_map/stack_step/pallas_call | solution.py:545
  138.4 0.6 copy.25
  139.0 0.7 copy.26
  139.7 0.6 copy.27
  140.4 2.4 %copy.28 = bf16[1,64,5,64,128]{4,3,2,1,0:T(8,128)(2,1)} copy(bf16[1,64,5,64,128]{4,3,2,1,0:T(8,128)(2,1)S(1)} %bitcast.29) | data formatting | bytes 10485760

commit v3 on v2

v3 whole, which is shorter than its diff:
```python
import functools

import jax
import jax.numpy as jnp
from jax import lax
from jax.experimental import pallas as pl
from jax.experimental.pallas import tpu as pltpu
from jax.sharding import PartitionSpec as P

epsilon = 1e-05
MESH = pl.DeviceIdType.MESH
F32, BF16 = jnp.float32, jnp.bfloat16
SIDE = 4
NEAR = (0, 1, 3, 2)
FAR = (2, 1, 3, 0)
BLOCKS = 2
EARLY = (1, 3)


def silu(v):
    return v / (1.0 + jnp.exp(-v))


def softplus(v):
    return jnp.maximum(v, 0.0) + jnp.log1p(jnp.exp(-jnp.abs(v)))


def kernel(
    sections,
    hid_ref,
    gain_hbm,
    wzx_hbm,
    wbc_hbm,
    wdt_hbm,
    dtb_hbm,
    alog_hbm,
    dsk_hbm,
    cxw_hbm,
    cxb_hbm,
    cbw_hbm,
    cbb_hbm,
    ig_hbm,
    wout_hbm,
    cxs_hbm,
    cbs_hbm,
    ssm_hbm,
    sec_out,
    cx_out,
    cb_out,
    st,
    gain_ref,
    wdt_ref,
    dtb_ref,
    alog_ref,
    dsk_ref,
    cxw_ref,
    cxb_ref,
    cbw_ref,
    cbb_ref,
    ig_ref,
    cxs_ref,
    cbs_ref,
    w_all,
    w_o,
    hbuf,
    acc,
    wdt_pad,
    pre_bc,
    pre_x,
    par,
    q_buf,
    inner,
    stx,
    dec,
    b_buf,
    xf_buf,
    stx_t,
    send_buf,
    rs_buf,
    ag_src,
    init_buf,
    sh_buf,
    load_sem,
    small_sem,
    init_send,
    init_recv,
    rs_send,
    rs_recv,
    ag_send,
    ag_recv,
    sh_send,
    sh_recv,
):
    heads, streams, p_size = cxs_hbm.shape[1:]
    width, n2 = wbc_hbm.shape
    n_state = n2 // 2
    chunk = width // SIDE
    block = streams // BLOCKS
    rows = block // SIDE
    share = hid_ref.shape[1]
    team = SIDE * SIDE
    last = sections - 1

    sec = lax.axis_index("section")
    me = lax.axis_index("tensor")
    my_z = me // SIDE
    my_y = me % SIDE

    def dev(s, t):
        return {"section": s, "tensor": t}

    loads = [pltpu.make_async_copy(wbc_hbm, w_all.at[:, pl.ds(0, n2)], load_sem.at[0])]
    for h in range(heads):
        loads.append(
            pltpu.make_async_copy(
                wzx_hbm.at[h], w_all.at[:, pl.ds(n2 + 128 * h, 128)], load_sem.at[1 + h]
            )
        )
    at = 1 + heads
    for yy in range(SIDE):
        loads.append(
            pltpu.make_async_copy(
                wout_hbm.at[:, pl.ds(chunk * yy, chunk)], w_o.at[yy], load_sem.at[at + yy]
            )
        )
    at += SIDE
    loads.append(pltpu.make_async_copy(ssm_hbm, st, load_sem.at[at]))
    smalls = [
        pltpu.make_async_copy(a, b, small_sem.at[i])
        for i, (a, b) in enumerate(
            (
                (wdt_hbm, wdt_ref),
                (gain_hbm, gain_ref),
                (dtb_hbm, dtb_ref),
                (alog_hbm, alog_ref),
                (dsk_hbm, dsk_ref),
                (cxw_hbm, cxw_ref),
                (cxb_hbm, cxb_ref),
                (cbw_hbm, cbw_ref),
                (cbb_hbm, cbb_ref),
                (ig_hbm, ig_ref),
                (cxs_hbm, cxs_ref),
                (cbs_hbm, cbs_ref),
            )
        )
    ]

    barrier = pltpu.get_barrier_semaphore()

    def greet(j, carry):
        other = (me + j) % team

        @pl.when(j > 0)
        def _():
            pl.semaphore_signal(barrier, inc=1, device_id=dev(sec, other), device_id_type=MESH)

        @pl.when(sec > 0)
        def _():
            pl.semaphore_signal(barrier, inc=1, device_id=dev(sec - 1, other), device_id_type=MESH)

        @pl.when(sec < last)
        def _():
            pl.semaphore_signal(barrier, inc=1, device_id=dev(sec + 1, other), device_id_type=MESH)

        return carry

    for cp in smalls + loads:
        cp.start()
    lax.fori_loop(0, team, greet, 0)
    partners = team - 1 + jnp.where(sec > 0, team, 0) + jnp.where(sec < last, team, 0)
    pl.semaphore_wait(barrier, partners)

    def init_copy(dest):
        return pltpu.make_async_remote_copy(
            src_ref=hid_ref,
            dst_ref=init_buf.at[me],
            send_sem=init_send.at[dest],
            recv_sem=init_recv.at[me],
            device_id=dev(sec, dest),
            device_id_type=MESH,
        )

    def init_own():
        return pltpu.make_async_copy(hid_ref, init_buf.at[me], init_recv.at[me])

    @pl.when(sec == 0)
    def _():
        def go(j, carry):
            init_copy((me + j) % team).start()
            return carry

        lax.fori_loop(1, team, go, 0)
        init_own().start()

    for cp in smalls:
        cp.wait()
    wdt_pad[...] = jnp.zeros_like(wdt_pad)
    wdt_pad[0:heads, :] = wdt_ref[...].astype(F32)
    for h in range(1 + heads):
        loads[h].wait()
    for j in range(width // 128):
        blk = wdt_pad[:, 128 * j : 128 * j + 128]
        w_all[128 * j : 128 * j + 128, n2 + 128 * heads : n2 + 128 * heads + 128] = blk.T.astype(BF16)
    q_buf[...] = jnp.zeros_like(q_buf)
    cb_out[0] = cbs_ref[1]
    cb_out[1] = cbs_ref[2]
    cx_out[0] = cxs_ref[1]
    cx_out[1] = cxs_ref[2]
    cbw = cbw_ref[...]
    pre_bc[...] = (
        cbs_ref[0].astype(F32) * cbw[0:1]
        + cbs_ref[1].astype(F32) * cbw[1:2]
        + cbs_ref[2].astype(F32) * cbw[2:3]
        + cbb_ref[...]
    )
    pairs = (heads + 1) // 2

    def packed(get, k):
        a = get(2 * k)
        b = get(2 * k + 1) if 2 * k + 1 < heads else jnp.zeros_like(a)
        return jnp.concatenate([a, b], axis=1)

    def pre_of(h):
        w = cxw_ref[h]
        return (
            cxs_ref[0, h].astype(F32) * w[0:1]
            + cxs_ref[1, h].astype(F32) * w[1:2]
            + cxs_ref[2, h].astype(F32) * w[2:3]
            + cxb_ref[h]
        )

    for k in range(pairs):
        pre_x[k] = packed(pre_of, k)
        par[0, k] = packed(lambda h: cxw_ref[h][3:4], k)
        par[1, k] = packed(lambda h: ig_ref[h], k)
        par[2, k] = packed(
            lambda h: jnp.broadcast_to(dsk_ref[:, h : h + 1], (1, p_size)), k
        )
    pad = jnp.zeros((1, 128 - heads), F32)
    dtb = jnp.concatenate([dtb_ref[...], pad], axis=1)
    neg_a = -jnp.exp(jnp.concatenate([alog_ref[...], pad], axis=1))

    @pl.when(sec == 0)
    def _():
        def wait_one(k, carry):
            pltpu.make_async_copy(hid_ref, init_buf.at[k], init_recv.at[k]).wait()
            return carry

        lax.fori_loop(0, team, wait_one, 0)
        for yy in range(SIDE):
            parts = [init_buf[SIDE * yy + i].astype(F32) for i in range(SIDE)]
            whole = jnp.concatenate(parts, axis=1)
            for blk in range(BLOCKS):
                for zz in range(SIDE):
                    at_row = blk * block + zz * rows
                    hbuf[blk, yy, zz] = whole[at_row : at_row + rows].astype(BF16)

    def ag_copy(blk, src_t, dest):
        return pltpu.make_async_remote_copy(
            src_ref=ag_src.at[blk],
            dst_ref=hbuf.at[blk, src_t % SIDE, src_t // SIDE],
            send_sem=ag_send.at[blk, dest],
            recv_sem=ag_recv.at[blk, src_t],
            device_id=dev(jnp.minimum(sec + 1, last), dest),
            device_id_type=MESH,
        )

    def rs_copy(blk, src_t, dest, yy, zz):
        return pltpu.make_async_remote_copy(
            src_ref=send_buf.at[blk, yy, zz],
            dst_ref=rs_buf.at[blk, src_t],
            send_sem=rs_send.at[blk, dest],
            recv_sem=rs_recv.at[blk, src_t],
            device_id=dev(sec, dest),
            device_id_type=MESH,
        )

    def rs_own(blk):
        return pltpu.make_async_copy(
            send_buf.at[blk, my_y, my_z], rs_buf.at[blk, me], rs_recv.at[blk, me]
        )

    for cp in loads[1 + heads :]:
        cp.wait()
    lane = lax.broadcasted_iota(jnp.int32, (block, 128), 1)
    low = lane < p_size
    hp = heads * p_size
    dt0 = n2 + 128 * heads
    group = 16
    row = lax.broadcasted_iota(jnp.int32, (group, n_state), 0)

    def layer(blk, carry):
        here = pl.ds(pl.multiple_of(blk * block, block), block)

        sq = jnp.zeros((block, 128), F32)
        for off in NEAR:
            yy = (my_y + off) % SIDE

            @pl.when(sec > 0)
            def _():
                for zo in NEAR:
                    ag_copy(blk, ((my_z + zo) % SIDE) * SIDE + yy, me).wait_recv()

            hv = jnp.concatenate([hbuf[blk, yy, zz].astype(F32) for zz in range(SIDE)], axis=0)
            for i in range(chunk // 128):
                part = hv[:, 128 * i : 128 * i + 128]
                sq = sq + part * part
            start = pl.multiple_of(yy * chunk, chunk)
            hg = (hv * gain_ref[:, pl.ds(start, chunk)]).astype(BF16)
            term = jnp.dot(hg, w_all[pl.ds(start, chunk), :], preferred_element_type=F32)
            if off == NEAR[0]:
                acc[...] = term
            else:
                acc[...] += term
        r = lax.rsqrt(jnp.sum(sq, axis=1, keepdims=True) * (1.0 / width) + epsilon)

        bcf = (acc[:, 0:n2] * r).astype(BF16)
        cb_out[2, here, :] = bcf
        bcv = silu(pre_bc[here, :] + bcf.astype(F32) * cbw_ref[3:4, :])
        b_in = bcv[:, 0:n_state]
        c_out = bcv[:, n_state:n2]
        b_buf[here, :] = b_in
        bd = jnp.sum(b_in * c_out, axis=1, keepdims=True)

        for g in range(block // group):
            c16 = c_out[group * g : group * g + group]
            base = blk * block + group * g
            total = None
            for i in range(0, group, 2):
                lhs = jnp.concatenate(
                    [jnp.where(row == i, c16, 0.0), jnp.where(row == i + 1, c16, 0.0)], axis=1
                ).astype(BF16)
                rhs = jnp.concatenate([st[base + i], st[base + i + 1]], axis=1)
                term = lax.dot_general(
                    lhs, rhs, (((1,), (1,)), ((), ())), preferred_element_type=F32
                )
                total = term if total is None else total + term
            q_buf[group * g : group * g + group, 0:hp] = total

        step = softplus(acc[:, dt0 : dt0 + 128] * r + dtb)
        decay = jnp.exp(step * neg_a)

        def each(v):
            return [jnp.broadcast_to(v[:, h : h + 1], (block, 128)) for h in range(heads)]

        steps, decays = each(step), each(decay)
        for h in range(heads):
            dec[h, here, :] = decays[h]

        def spread(v, k):
            return jnp.where(low, v[2 * k], v[min(2 * k + 1, heads - 1)])

        sq = jnp.zeros((block, 128), F32)
        for k in range(pairs):
            a = acc[:, n2 + 256 * k : n2 + 256 * k + 128]
            if 2 * k + 1 < heads:
                b = acc[:, n2 + 256 * k + 128 : n2 + 256 * k + 256]
            else:
                b = jnp.zeros_like(a)
            x_new = jnp.where(low, pltpu.roll(a, p_size, 1), b)
            z_new = jnp.where(low, a, pltpu.roll(b, p_size, 1))
            xf = (x_new * r).astype(BF16)
            xf_buf[k, here, :] = xf
            xc = silu(pre_x[k, here, :] + xf.astype(F32) * par[0, k])
            sx = spread(steps, k) * xc
            stx[k, here, :] = sx
            q = q_buf[:, 128 * k : 128 * k + 128]
            y_out = spread(decays, k) * q + sx * bd + par[2, k] * xc
            gated = y_out * silu(z_new * r)
            sq = sq + gated * gated
            inner[:, 128 * k : 128 * k + 128] = (gated * par[1, k]).astype(BF16)
        squares = jnp.sum(sq, axis=1, keepdims=True)
        hi = squares.astype(BF16).astype(F32)
        lo = squares - hi
        sq_tile = jnp.where(lane == 0, hi, jnp.where(lane == 1, lo, 0.0))

        for yo in FAR:
            yy = (my_y + yo) % SIDE
            part = jnp.dot(inner[:, 0:hp], w_o[yy], preferred_element_type=F32)
            whole = jnp.concatenate([part, sq_tile], axis=1)
            for zz in range(SIDE):
                send_buf[blk, yy, zz] = whole[rows * zz : rows * zz + rows].astype(BF16)
            for zo in FAR:
                zz = (my_z + zo) % SIDE
                if yo == 0 and zo == 0:
                    rs_own(blk).start()
                else:
                    rs_copy(blk, me, zz * SIDE + yy, yy, zz).start()
        return carry

    lax.fori_loop(0, BLOCKS, layer, 0)

    octet = 8
    per_block = block // octet

    def turn():
        zeros = jnp.zeros((128 - streams, 128), F32)
        for k in range(pairs):
            stx_t[128 * k : 128 * k + 128] = jnp.concatenate([stx[k], zeros], axis=0).T

    def update(g, carry):
        shift = (128 - g * octet) % 128
        span8 = pl.ds(pl.multiple_of(g * octet, octet), octet)
        b8 = b_buf[span8, :]
        for h in range(heads):
            span = slice(p_size * h, p_size * h + p_size)
            sx_r = pltpu.roll(stx_t[span, :], shift, 1)
            d8 = dec[h, span8, :]
            for i in range(octet):
                old = st[g * octet + i, span, :].astype(F32)
                new = d8[i : i + 1] * old + jnp.broadcast_to(
                    sx_r[:, i : i + 1], (p_size, 128)
                ) * b8[i : i + 1]
                st[g * octet + i, span, :] = new.astype(BF16)
        return carry

    def sh_copy(blk, src_z, j):
        return pltpu.make_async_remote_copy(
            src_ref=ag_src.at[blk],
            dst_ref=sh_buf.at[blk, src_z],
            send_sem=sh_send.at[blk, j],
            recv_sem=sh_recv.at[blk, src_z],
            device_id=dev(sec, my_y * SIDE + j),
            device_id_type=MESH,
        )

    turn()
    for blk in range(BLOCKS):
        lax.fori_loop(EARLY[blk - 1] if blk else 0, EARLY[blk], update, 0)

        tot = jnp.zeros((rows, chunk + 128), F32)
        for yo in NEAR:
            for zo in NEAR:
                src = ((my_z + zo) % SIDE) * SIDE + (my_y + yo) % SIDE
                if yo == 0 and zo == 0:
                    rs_own(blk).wait()
                else:
                    rs_copy(blk, src, me, my_y, my_z).wait_recv()
                tot = tot + rs_buf[blk, src].astype(F32)
        scale = lax.rsqrt(
            jnp.sum(tot[:, chunk : chunk + 128], axis=1, keepdims=True) * (1.0 / (hp * team))
            + epsilon
        )
        mine = hbuf[blk, my_y, my_z].astype(F32)
        ag_src[blk] = (mine + tot[:, 0:chunk] * scale).astype(BF16)

        @pl.when(sec < last)
        def _():
            for yo in FAR:
                for zo in FAR:
                    ag_copy(blk, me, ((my_z + zo) % SIDE) * SIDE + (my_y + yo) % SIDE).start()

        for j in range(SIDE):
            own = my_y * SIDE + j == me

            @pl.when(own)
            def _():
                pltpu.make_async_copy(
                    ag_src.at[blk], sh_buf.at[blk, my_z], sh_recv.at[blk, my_z]
                ).start()

            @pl.when(jnp.logical_not(own))
            def _():
                sh_copy(blk, my_z, j).start()

    lax.fori_loop(EARLY[-1], streams // octet, update, 0)

    for h in range(heads):
        xf = xf_buf[h // 2].astype(F32)
        cx_out[2, h] = xf[:, p_size * (h % 2) : p_size * (h % 2) + p_size].astype(BF16)

    for blk in range(BLOCKS):
        for zz in range(SIDE):
            sh_copy(blk, zz, 0).wait_recv()
    for yy in range(SIDE):

        @pl.when(my_y == yy)
        def _():
            whole = jnp.concatenate(
                [
                    sh_buf[blk, zz].astype(F32)
                    for blk in range(BLOCKS)
                    for zz in range(SIDE)
                ],
                axis=0,
            )
            sec_out[...] = whole[:, share * yy : share * yy + share].astype(BF16)

    for blk in range(BLOCKS):
        for yo in FAR:
            for zo in FAR:
                dest = ((my_z + zo) % SIDE) * SIDE + (my_y + yo) % SIDE
                if not (yo == 0 and zo == 0):
                    rs_copy(blk, me, dest, my_y, my_z).wait_send()

        @pl.when(sec < last)
        def _():
            for dest in range(team):
                ag_copy(blk, me, dest).wait_send()

        for j in range(SIDE):

            @pl.when(my_y * SIDE + j != me)
            def _():
                sh_copy(blk, my_z, j).wait_send()

    @pl.when(sec == 0)
    def _():
        def sent(j, carry):
            init_copy((me + j) % team).wait_send()
            return carry

        lax.fori_loop(1, team, sent, 0)


def shards(
    hidden_in,
    pre_gain,
    w_zx,
    w_bc,
    w_dt,
    dt_bias,
    a_log,
    d_skip,
    conv_x_weight,
    conv_x_bias,
    conv_bc_weight,
    conv_bc_bias,
    inner_gain,
    w_out,
    conv_x_state,
    conv_bc_state,
    ssm_state,
    sections,
):
    streams, share = hidden_in.shape
    _, heads, p_size, width = w_out.shape
    n2 = w_bc.shape[2]
    n_state = n2 // 2
    team = SIDE * SIDE
    chunk, block = width // SIDE, streams // BLOCKS
    rows = block // SIDE
    hp = heads * p_size
    cols = n2 + 128 * heads + 128
    pairs = (heads + 1) // 2
    args = (
        hidden_in,
        pre_gain,
        jnp.transpose(w_zx[0], (1, 0, 2)),
        w_bc[0],
        jnp.transpose(w_dt[0], (1, 0)),
        dt_bias,
        a_log,
        d_skip,
        jnp.transpose(conv_x_weight[0], (1, 0, 2)),
        jnp.transpose(conv_x_bias, (1, 0, 2)),
        conv_bc_weight[0],
        conv_bc_bias,
        jnp.transpose(inner_gain, (1, 0, 2)),
        w_out[0].reshape(hp, width),
        jnp.transpose(conv_x_state[0], (1, 2, 0, 3)),
        jnp.transpose(conv_bc_state[0], (1, 0, 2)),
        ssm_state[0].reshape(streams, hp, n_state),
    )
    vmem = pl.BlockSpec(memory_space=pltpu.VMEM)
    hbm = pl.BlockSpec(memory_space=pltpu.HBM)
    small = (1, 4, 5, 6, 7, 8, 9, 10, 11, 12, 14, 15)
    dma = pltpu.SemaphoreType.DMA
    sec_new, cx_new, cb_new, ssm_new = pl.pallas_call(
        functools.partial(kernel, sections),
        out_shape=(
            jax.ShapeDtypeStruct((streams, share), BF16),
            jax.ShapeDtypeStruct((3, heads, streams, p_size), BF16),
            jax.ShapeDtypeStruct((3, streams, n2), BF16),
            jax.ShapeDtypeStruct((streams, hp, n_state), BF16),
        ),
        in_specs=[hbm] * len(args),
        out_specs=(vmem, vmem, vmem, vmem),
        scratch_shapes=[pltpu.VMEM(args[i].shape, args[i].dtype) for i in small]
        + [
            pltpu.VMEM((width, cols), BF16),
            pltpu.VMEM((SIDE, hp, chunk), BF16),
            pltpu.VMEM((BLOCKS, SIDE, SIDE, rows, chunk), BF16),
            pltpu.VMEM((block, cols), F32),
            pltpu.VMEM((128, width), F32),
            pltpu.VMEM((streams, n2), F32),
            pltpu.VMEM((pairs, streams, 128), F32),
            pltpu.VMEM((3, pairs, 1, 128), F32),
            pltpu.VMEM((block, 128 * pairs), F32),
            pltpu.VMEM((block, 128 * pairs), BF16),
            pltpu.VMEM((pairs, streams, 128), F32),
            pltpu.VMEM((heads, streams, 128), F32),
            pltpu.VMEM((streams, n_state), F32),
            pltpu.VMEM((pairs, streams, 128), BF16),
            pltpu.VMEM((128 * pairs, 128), F32),
            pltpu.VMEM((BLOCKS, SIDE, SIDE, rows, chunk + 128), BF16),
            pltpu.VMEM((BLOCKS, team, rows, chunk + 128), BF16),
            pltpu.VMEM((BLOCKS, rows, chunk), BF16),
            pltpu.VMEM((team, streams, share), BF16),
            pltpu.VMEM((BLOCKS, SIDE, rows, chunk), BF16),
            dma((1 + heads + SIDE + 1,)),
            dma((len(small),)),
            dma((team,)),
            dma((team,)),
            dma((BLOCKS, team)),
            dma((BLOCKS, team)),
            dma((BLOCKS, team)),
            dma((BLOCKS, team)),
            dma((BLOCKS, SIDE)),
            dma((BLOCKS, SIDE)),
        ],
        compiler_params=pltpu.CompilerParams(
            collective_id=0, has_side_effects=True, vmem_limit_bytes=40 * 1024 * 1024
        ),
        name="stack_step",
    )(*[pltpu.with_memory_space_constraint(a, pltpu.HBM) for a in args])
    return (
        sec_new[None],
        jnp.transpose(cx_new, (2, 0, 1, 3))[None],
        jnp.transpose(cb_new, (1, 0, 2))[None],
        ssm_new.reshape(ssm_state.shape),
    )


def solution(mesh):
    placed = (
        P(None, "tensor"),
        P("section", None),
        P("section", None, "tensor", None),
        P("section", None, None),
        P("section", None, "tensor"),
        P("section", "tensor"),
        P("section", "tensor"),
        P("section", "tensor"),
        P("section", None, "tensor", None),
        P("section", "tensor", None),
        P("section", None, None),
        P("section", None),
        P("section", "tensor", None),
        P("section", "tensor", None, None),
        P("section", None, None, "tensor", None),
        P("section", None, None, None),
        P("section", None, "tensor", None, None),
    )
    return jax.shard_map(
        functools.partial(shards, sections=mesh.shape["section"]),
        mesh=mesh,
        in_specs=placed,
        out_specs=(
            P("section", None, "tensor"),
            P("section", None, None, "tensor", None),
            P("section", None, None, None),
            P("section", None, "tensor", None, None),
        ),
        check_vma=False,
    )
```

time: 143 us -> 116 us (0.81)
  Pallas kernels: 138 us -> 111 us
    pallas_call x1, Pallas kernels: 138 us -> 111 us  [shards(): pl.pallas_call(functools.partial(kernel, sections), out_shape=(jax.ShapeD...]
where the time goes in v3:
time: 116 us
  Pallas kernels  111 us (96%)
  local copies, waits for them, and re-layouts  4.31 us (4%)
    pallas_call x1, Pallas kernels, shards(): pl.pallas_call(functools.partial(kernel, sections), out_shape=(jax.ShapeD...  111 us
    unnamed x4, local copies, waits for them, and re-layouts  4.31 us

profile of v3, /device:TPU:7, one launch (start us, length us, event | category | flops | bytes accessed | tf_op | source)
XLA Modules:
  0.0 116.1 jit_solution(8910095343596060825)
XLA Ops:
  0.6 111.2 %stack_step.1 = (bf16[64,160]{1,0:T(8,128)(2,1)S(1)}, bf16[3,5,64,64]{3,2,1,0:T(8,128)(2,1)S(1)}, bf16[3,64,256]{2,1,0:T(8,128)(2,1)S(1)}, bf16[64,320,128]{2,1,0:T(8,128)(2,1)S(1)}) custom-call(bf16[64,160]{1,0:T(8,128)(2,1)} %hid_ref.1, f32[1,2560]{1,0:T(1,128)} %gain_hbm.1, bf16[5,2560,128]{2,1,0:T(8,128)(2,1)} %bitcast.34, bf16[2560,256]{1,0:T(8,128)(2,1)} %bitcast.36, ...), custom_call_target="tpu_custom_call" | custom-call | tf_op jit(solution)/shard_map/stack_step/pallas_call | solution.py:569
  111.8 0.6 copy.25
  112.4 0.7 copy.26
  113.1 0.6 copy.27
  113.8 2.4 %copy.28 = bf16[1,64,5,64,128]{4,3,2,1,0:T(8,128)(2,1)} copy(bf16[1,64,5,64,128]{4,3,2,1,0:T(8,128)(2,1)S(1)} %bitcast.29) | data formatting | bytes 10485760

commit v4 on v3

--- a/solution.py
+++ b/solution.py
@@ -13,6 +13,7 @@
 SIDE = 4
 NEAR = (0, 1, 3, 2)
 FAR = (2, 1, 3, 0)
+PIECES = 4
 BLOCKS = 2
 EARLY = (1, 3)
 
@@ -27,7 +28,7 @@
 
 def kernel(
     sections,
-    hid_ref,
+    hid_hbm,
     gain_hbm,
     wzx_hbm,
     wbc_hbm,
@@ -48,6 +49,8 @@
     cx_out,
     cb_out,
     st,
+    hid_ref,
+    pack,
     gain_ref,
     wdt_ref,
     dtb_ref,
@@ -80,6 +83,7 @@
     ag_src,
     init_buf,
     sh_buf,
+    hid_sem,
     load_sem,
     small_sem,
     init_send,
@@ -97,7 +101,7 @@
     chunk = width // SIDE
     block = streams // BLOCKS
     rows = block // SIDE
-    share = hid_ref.shape[1]
+    share = hid_hbm.shape[1]
     team = SIDE * SIDE
     last = sections - 1
 
@@ -147,50 +151,62 @@
 
     barrier = pltpu.get_barrier_semaphore()
 
-    def greet(j, carry):
-        other = (me + j) % team
-
-        @pl.when(j > 0)
-        def _():
-            pl.semaphore_signal(barrier, inc=1, device_id=dev(sec, other), device_id_type=MESH)
-
-        @pl.when(sec > 0)
-        def _():
+    ring = [
+        ((my_z + zo) % SIDE) * SIDE + (my_y + yo) % SIDE for yo in FAR for zo in FAR
+    ]
+
+    for other in ring[:-1]:
+        pl.semaphore_signal(barrier, inc=1, device_id=dev(sec, other), device_id_type=MESH)
+
+    @pl.when(sec > 0)
+    def _():
+        for other in ring:
             pl.semaphore_signal(barrier, inc=1, device_id=dev(sec - 1, other), device_id_type=MESH)
 
-        @pl.when(sec < last)
-        def _():
+    @pl.when(sec < last)
+    def _():
+        for other in ring:
             pl.semaphore_signal(barrier, inc=1, device_id=dev(sec + 1, other), device_id_type=MESH)
 
-        return carry
-
+    hid_copy = pltpu.make_async_copy(hid_hbm, hid_ref, hid_sem)
+    hid_copy.start()
     for cp in smalls + loads:
         cp.start()
-    lax.fori_loop(0, team, greet, 0)
+
+    hid_copy.wait()
+    for blk in range(BLOCKS):
+        parts = [
+            hid_ref[blk * block + rows * zz : blk * block + rows * zz + rows, :].astype(F32)
+            if rows % 16 == 0
+            else hid_ref[blk * block : blk * block + block, :].astype(F32)[rows * zz : rows * zz + rows]
+            for zz in range(SIDE)
+        ]
+        pack[blk] = jnp.concatenate(parts, axis=1).astype(BF16)
+
     partners = team - 1 + jnp.where(sec > 0, team, 0) + jnp.where(sec < last, team, 0)
     pl.semaphore_wait(barrier, partners)
 
-    def init_copy(dest):
+    def init_copy(blk, src_t, dest):
         return pltpu.make_async_remote_copy(
-            src_ref=hid_ref,
-            dst_ref=init_buf.at[me],
-            send_sem=init_send.at[dest],
-            recv_sem=init_recv.at[me],
+            src_ref=pack.at[blk],
+            dst_ref=init_buf.at[blk, src_t],
+            send_sem=init_send.at[blk, dest],
+            recv_sem=init_recv.at[blk, src_t],
             device_id=dev(sec, dest),
             device_id_type=MESH,
         )
 
-    def init_own():
-        return pltpu.make_async_copy(hid_ref, init_buf.at[me], init_recv.at[me])
+    def init_own(blk):
+        return pltpu.make_async_copy(
+            pack.at[blk], init_buf.at[blk, me], init_recv.at[blk, me]
+        )
 
     @pl.when(sec == 0)
     def _():
-        def go(j, carry):
-            init_copy((me + j) % team).start()
-            return carry
-
-        lax.fori_loop(1, team, go, 0)
-        init_own().start()
+        for blk in range(BLOCKS):
+            for other in ring[:-1]:
+                init_copy(blk, me, other).start()
+            init_own(blk).start()
 
     for cp in smalls:
         cp.wait()
@@ -240,21 +256,6 @@
     dtb = jnp.concatenate([dtb_ref[...], pad], axis=1)
     neg_a = -jnp.exp(jnp.concatenate([alog_ref[...], pad], axis=1))
 
-    @pl.when(sec == 0)
-    def _():
-        def wait_one(k, carry):
-            pltpu.make_async_copy(hid_ref, init_buf.at[k], init_recv.at[k]).wait()
-            return carry
-
-        lax.fori_loop(0, team, wait_one, 0)
-        for yy in range(SIDE):
-            parts = [init_buf[SIDE * yy + i].astype(F32) for i in range(SIDE)]
-            whole = jnp.concatenate(parts, axis=1)
-            for blk in range(BLOCKS):
-                for zz in range(SIDE):
-                    at_row = blk * block + zz * rows
-                    hbuf[blk, yy, zz] = whole[at_row : at_row + rows].astype(BF16)
-
     def ag_copy(blk, src_t, dest):
         return pltpu.make_async_remote_copy(
             src_ref=ag_src.at[blk],
@@ -291,6 +292,18 @@
 
     def layer(blk, carry):
         here = pl.ds(pl.multiple_of(blk * block, block), block)
+
+        @pl.when(sec == 0)
+        def _():
+            for other in ring[:-1]:
+                init_copy(blk, other, me).wait_recv()
+            init_own(blk).wait()
+            for yy in range(SIDE):
+                parts = [init_buf[blk, SIDE * yy + i].astype(F32) for i in range(SIDE)]
+                for zz in range(SIDE):
+                    hbuf[blk, yy, zz] = jnp.concatenate(
+                        [part[:, share * zz : share * zz + share] for part in parts], axis=1
+                    ).astype(BF16)
 
         sq = jnp.zeros((block, 128), F32)
         for off in NEAR:
@@ -506,11 +519,23 @@
 
     @pl.when(sec == 0)
     def _():
-        def sent(j, carry):
-            init_copy((me + j) % team).wait_send()
-            return carry
-
-        lax.fori_loop(1, team, sent, 0)
+        for blk in range(BLOCKS):
+            for other in ring[:-1]:
+                init_copy(blk, me, other).wait_send()
+
+
+def write_out(a_in, b_in, c_in, d_in, a_out, b_out, c_out, d_out, sems):
+    size = d_in.shape[0] // PIECES
+    copies = [
+        pltpu.make_async_copy(d_in.at[pl.ds(size * i, size)], d_out.at[pl.ds(size * i, size)], sems.at[3 + i])
+        for i in range(PIECES)
+    ]
+    for i, (x, y) in enumerate(((a_in, a_out), (b_in, b_out), (c_in, c_out))):
+        copies.append(pltpu.make_async_copy(x, y, sems.at[i]))
+    for cp in copies:
+        cp.start()
+    for cp in copies:
+        cp.wait()
 
 
 def shards(
@@ -576,7 +601,11 @@
         ),
         in_specs=[hbm] * len(args),
         out_specs=(vmem, vmem, vmem, vmem),
-        scratch_shapes=[pltpu.VMEM(args[i].shape, args[i].dtype) for i in small]
+        scratch_shapes=[
+            pltpu.VMEM((streams, share), BF16),
+            pltpu.VMEM((BLOCKS, rows, chunk), BF16),
+        ]
+        + [pltpu.VMEM(args[i].shape, args[i].dtype) for i in small]
         + [
             pltpu.VMEM((width, cols), BF16),
             pltpu.VMEM((SIDE, hp, chunk), BF16),
@@ -596,12 +625,13 @@
             pltpu.VMEM((BLOCKS, SIDE, SIDE, rows, chunk + 128), BF16),
             pltpu.VMEM((BLOCKS, team, rows, chunk + 128), BF16),
             pltpu.VMEM((BLOCKS, rows, chunk), BF16),
-            pltpu.VMEM((team, streams, share), BF16),
+            pltpu.VMEM((BLOCKS, team, rows, chunk), BF16),
             pltpu.VMEM((BLOCKS, SIDE, rows, chunk), BF16),
+            dma(()),
             dma((1 + heads + SIDE + 1,)),
             dma((len(small),)),
-            dma((team,)),
-            dma((team,)),
+            dma((BLOCKS, team)),
+            dma((BLOCKS, team)),
             dma((BLOCKS, team)),
             dma((BLOCKS, team)),
             dma((BLOCKS, team)),
@@ -614,6 +644,16 @@
         ),
         name="stack_step",
     )(*[pltpu.with_memory_space_constraint(a, pltpu.HBM) for a in args])
+    results = (sec_new, cx_new, cb_new, ssm_new)
+    sec_new, cx_new, cb_new, ssm_new = pl.pallas_call(
+        write_out,
+        out_shape=tuple(jax.ShapeDtypeStruct(a.shape, a.dtype) for a in results),
+        in_specs=[vmem] * 4,
+        out_specs=(pl.BlockSpec(memory_space=pltpu.HBM),) * 4,
+        scratch_shapes=[dma((3 + PIECES,))],
+        compiler_params=pltpu.CompilerParams(vmem_limit_bytes=16 * 1024 * 1024),
+        name="write_out",
+    )(*results)
     return (
         sec_new[None],
         jnp.transpose(cx_new, (2, 0, 1, 3))[None],

time: 116 us -> 112 us (0.966)
  local copies, waits for them, and re-layouts: 4.31 us -> 0 us
    unnamed x4 -> x0, local copies, waits for them, and re-layouts: 4.31 us -> none
    pallas_call x0 -> x1, Pallas kernels: none -> 2.51 us  [shards(): pl.pallas_call(write_out, out_shape=tuple((jax.ShapeDtypeStruct(a.shape,...]
    pallas_call x1, Pallas kernels: 111 us -> 109 us  [shards(): pl.pallas_call(functools.partial(kernel, sections), out_shape=(jax.ShapeD...]
where the time goes in v4:
time: 112 us
  Pallas kernels  112 us (100%)
    pallas_call x1, Pallas kernels, shards(): pl.pallas_call(functools.partial(kernel, sections), out_shape=(jax.ShapeD...  109 us
    pallas_call x1, Pallas kernels, shards(): pl.pallas_call(write_out, out_shape=tuple((jax.ShapeDtypeStruct(a.shape,...  2.51 us

profile of v4, /device:TPU:7, one launch (start us, length us, event | category | flops | bytes accessed | tf_op | source)
XLA Modules:
  0.0 112.3 jit_solution(5681765755208973373)
XLA Ops:
  0.6 109.1 %stack_step.1 = (bf16[64,160]{1,0:T(8,128)(2,1)S(1)}, bf16[3,5,64,64]{3,2,1,0:T(8,128)(2,1)S(1)}, bf16[3,64,256]{2,1,0:T(8,128)(2,1)S(1)}, bf16[64,320,128]{2,1,0:T(8,128)(2,1)S(1)}) custom-call(bf16[64,160]{1,0:T(8,128)(2,1)} %hid_hbm.1, f32[1,2560]{1,0:T(1,128)} %gain_hbm.1, bf16[5,2560,128]{2,1,0:T(8,128)(2,1)} %bitcast.30, bf16[2560,256]{1,0:T(8,128)(2,1)} %bitcast.32, ...), custom_call_target="tpu_custom_call" | custom-call | tf_op jit(solution)/shard_map/stack_step/pallas_call | solution.py:594
  109.8 2.5 %write_out.1 = (bf16[64,160]{1,0:T(8,128)(2,1)}, bf16[3,5,64,64]{3,2,1,0:T(8,128)(2,1)}, bf16[3,64,256]{2,1,0:T(8,128)(2,1)}, bf16[64,320,128]{2,1,0:T(8,128)(2,1)}) custom-call(bf16[64,160]{1,0:T(8,128)(2,1)S(1)} %get-tuple-element.12.a_in, bf16[3,5,64,64]{3,2,1,0:T(8,128)(2,1)S(1)} %get-tuple-element.13.b_in, ...), custom_call_target="tpu_custom_call" | custom-call | tf_op jit(solution)/shard_map/write_out/pallas_call | solution.py:648

commit v5 on v4

--- a/solution.py
+++ b/solution.py
@@ -15,7 +15,7 @@
 FAR = (2, 1, 3, 0)
 PIECES = 4
 BLOCKS = 2
-EARLY = (1, 3)
+EARLY = (2, 6)
 
 
 def silu(v):
@@ -83,6 +83,9 @@
     ag_src,
     init_buf,
     sh_buf,
+    send_end,
+    sum_end,
+    end_buf,
     hid_sem,
     load_sem,
     small_sem,
@@ -279,6 +282,21 @@
     def rs_own(blk):
         return pltpu.make_async_copy(
             send_buf.at[blk, my_y, my_z], rs_buf.at[blk, me], rs_recv.at[blk, me]
+        )
+
+    def end_copy(blk, src_t, zz, j):
+        return pltpu.make_async_remote_copy(
+            src_ref=send_end.at[blk, zz, j],
+            dst_ref=sum_end.at[blk, src_t],
+            send_sem=rs_send.at[blk, zz * SIDE + j],
+            recv_sem=rs_recv.at[blk, src_t],
+            device_id=dev(sec, zz * SIDE + j),
+            device_id_type=MESH,
+        )
+
+    def end_own(blk):
+        return pltpu.make_async_copy(
+            send_end.at[blk, my_z, my_y], sum_end.at[blk, me], rs_recv.at[blk, me]
         )
 
     for cp in loads[1 + heads :]:
@@ -388,17 +406,34 @@
         sq_tile = jnp.where(lane == 0, hi, jnp.where(lane == 1, lo, 0.0))
 
         for yo in FAR:
-            yy = (my_y + yo) % SIDE
+            yy = (jnp.where(sec < last, my_y, my_z) + yo) % SIDE
             part = jnp.dot(inner[:, 0:hp], w_o[yy], preferred_element_type=F32)
-            whole = jnp.concatenate([part, sq_tile], axis=1)
-            for zz in range(SIDE):
-                send_buf[blk, yy, zz] = whole[rows * zz : rows * zz + rows].astype(BF16)
-            for zo in FAR:
-                zz = (my_z + zo) % SIDE
-                if yo == 0 and zo == 0:
-                    rs_own(blk).start()
-                else:
-                    rs_copy(blk, me, zz * SIDE + yy, yy, zz).start()
+
+            @pl.when(sec < last)
+            def _():
+                whole = jnp.concatenate([part, sq_tile], axis=1)
+                for zz in range(SIDE):
+                    send_buf[blk, yy, zz] = whole[rows * zz : rows * zz + rows].astype(BF16)
+                for zo in FAR:
+                    zz = (my_z + zo) % SIDE
+                    if yo == 0 and zo == 0:
+                        rs_own(blk).start()
+                    else:
+                        rs_copy(blk, me, zz * SIDE + yy, yy, zz).start()
+
+            @pl.when(sec == last)
+            def _():
+                for j in range(SIDE):
+                    send_end[blk, yy, j] = jnp.concatenate(
+                        [part[:, 128 * j : 128 * j + 256], sq_tile], axis=1
+                    ).astype(BF16)
+                for jo in FAR:
+                    j = (my_y + jo) % SIDE
+                    if yo == 0 and jo == 0:
+                        end_own(blk).start()
+                    else:
+                        end_copy(blk, me, yy, j).start()
+
         return carry
 
     lax.fori_loop(0, BLOCKS, layer, 0)
@@ -409,22 +444,29 @@
     def turn():
         zeros = jnp.zeros((128 - streams, 128), F32)
         for k in range(pairs):
-            stx_t[128 * k : 128 * k + 128] = jnp.concatenate([stx[k], zeros], axis=0).T
+            turned = jnp.concatenate([stx[k], zeros], axis=0).T
+            stx_t[128 * k : 128 * k + 128] = turned[:, 0:streams].astype(BF16)
+
+    at_stream = lax.broadcasted_iota(jnp.int32, (streams, n_state), 0)
 
     def update(g, carry):
-        shift = (128 - g * octet) % 128
         span8 = pl.ds(pl.multiple_of(g * octet, octet), octet)
         b8 = b_buf[span8, :]
-        for h in range(heads):
-            span = slice(p_size * h, p_size * h + p_size)
-            sx_r = pltpu.roll(stx_t[span, :], shift, 1)
-            d8 = dec[h, span8, :]
-            for i in range(octet):
-                old = st[g * octet + i, span, :].astype(F32)
-                new = d8[i : i + 1] * old + jnp.broadcast_to(
-                    sx_r[:, i : i + 1], (p_size, 128)
-                ) * b8[i : i + 1]
-                st[g * octet + i, span, :] = new.astype(BF16)
+        for i in range(0, octet, 2):
+            rhs = jnp.concatenate(
+                [jnp.where(at_stream == g * octet + i + e, b8[i + e : i + e + 1], 0.0) for e in (0, 1)],
+                axis=1,
+            ).astype(BF16)
+            more = jnp.dot(stx_t[0:hp, :], rhs, preferred_element_type=F32)
+            for e in (0, 1):
+                for h in range(heads):
+                    span = slice(p_size * h, p_size * h + p_size)
+                    old = st[g * octet + i + e, span, :].astype(F32)
+                    new = (
+                        dec[h, span8, :][i + e : i + e + 1] * old
+                        + more[span, n_state * e : n_state * e + n_state]
+                    )
+                    st[g * octet + i + e, span, :] = new.astype(BF16)
         return carry
 
     def sh_copy(blk, src_z, j):
@@ -441,40 +483,70 @@
     for blk in range(BLOCKS):
         lax.fori_loop(EARLY[blk - 1] if blk else 0, EARLY[blk], update, 0)
 
-        tot = jnp.zeros((rows, chunk + 128), F32)
-        for yo in NEAR:
-            for zo in NEAR:
-                src = ((my_z + zo) % SIDE) * SIDE + (my_y + yo) % SIDE
-                if yo == 0 and zo == 0:
-                    rs_own(blk).wait()
-                else:
-                    rs_copy(blk, src, me, my_y, my_z).wait_recv()
-                tot = tot + rs_buf[blk, src].astype(F32)
-        scale = lax.rsqrt(
-            jnp.sum(tot[:, chunk : chunk + 128], axis=1, keepdims=True) * (1.0 / (hp * team))
-            + epsilon
-        )
-        mine = hbuf[blk, my_y, my_z].astype(F32)
-        ag_src[blk] = (mine + tot[:, 0:chunk] * scale).astype(BF16)
-
         @pl.when(sec < last)
         def _():
-            for yo in FAR:
-                for zo in FAR:
-                    ag_copy(blk, me, ((my_z + zo) % SIDE) * SIDE + (my_y + yo) % SIDE).start()
-
-        for j in range(SIDE):
-            own = my_y * SIDE + j == me
-
-            @pl.when(own)
-            def _():
-                pltpu.make_async_copy(
-                    ag_src.at[blk], sh_buf.at[blk, my_z], sh_recv.at[blk, my_z]
-                ).start()
-
-            @pl.when(jnp.logical_not(own))
-            def _():
-                sh_copy(blk, my_z, j).start()
+            tot = jnp.zeros((rows, chunk + 128), F32)
+            for yo in NEAR:
+                for zo in NEAR:
+                    src = ((my_z + zo) % SIDE) * SIDE + (my_y + yo) % SIDE
+                    if yo == 0 and zo == 0:
+                        rs_own(blk).wait()
+                    else:
+                        rs_copy(blk, src, me, my_y, my_z).wait_recv()
+                    tot = tot + rs_buf[blk, src].astype(F32)
+            scale = lax.rsqrt(
+                jnp.sum(tot[:, chunk : chunk + 128], axis=1, keepdims=True) * (1.0 / (hp * team))
+                + epsilon
+            )
+            mine = hbuf[blk, my_y, my_z].astype(F32)
+            ag_src[blk] = (mine + tot[:, 0:chunk] * scale).astype(BF16)
+
+            for other in ring:
+                ag_copy(blk, me, other).start()
+
+        @pl.when(sec == last)
+        def _():
+            tot = jnp.zeros((block, 384), F32)
+            for yo in NEAR:
+                for zo in NEAR:
+                    src = ((my_z + zo) % SIDE) * SIDE + (my_y + yo) % SIDE
+                    if yo == 0 and zo == 0:
+                        end_own(blk).wait()
+                    else:
+                        end_copy(blk, src, my_z, my_y).wait_recv()
+                    tot = tot + sum_end[blk, src].astype(F32)
+            scale = lax.rsqrt(
+                jnp.sum(tot[:, 256:384], axis=1, keepdims=True) * (1.0 / (hp * team)) + epsilon
+            )
+            window = pl.ds(pl.multiple_of(my_y * 128, 128), 256)
+            mine = jnp.concatenate(
+                [hbuf[blk, my_z, zz, :, window].astype(F32) for zz in range(SIDE)], axis=0
+            )
+            end_buf[...] = mine + tot[:, 0:256] * scale
+            for j in range(SIDE):
+
+                @pl.when(my_y == j)
+                def _():
+                    first = (share - 128) * j
+                    sec_out[blk * block : blk * block + block, :] = end_buf[...][
+                        :, first : first + share
+                    ].astype(BF16)
+
+    @pl.when(sec < last)
+    def _():
+        for blk in range(BLOCKS):
+            for j in range(SIDE):
+                own = my_y * SIDE + j == me
+
+                @pl.when(own)
+                def _():
+                    pltpu.make_async_copy(
+                        ag_src.at[blk], sh_buf.at[blk, my_z], sh_recv.at[blk, my_z]
+                    ).start()
+
+                @pl.when(jnp.logical_not(own))
+                def _():
+                    sh_copy(blk, my_z, j).start()
 
     lax.fori_loop(EARLY[-1], streams // octet, update, 0)
 
@@ -482,40 +554,43 @@
         xf = xf_buf[h // 2].astype(F32)
         cx_out[2, h] = xf[:, p_size * (h % 2) : p_size * (h % 2) + p_size].astype(BF16)
 
-    for blk in range(BLOCKS):
-        for zz in range(SIDE):
-            sh_copy(blk, zz, 0).wait_recv()
-    for yy in range(SIDE):
-
-        @pl.when(my_y == yy)
-        def _():
-            whole = jnp.concatenate(
-                [
-                    sh_buf[blk, zz].astype(F32)
-                    for blk in range(BLOCKS)
-                    for zz in range(SIDE)
-                ],
-                axis=0,
-            )
-            sec_out[...] = whole[:, share * yy : share * yy + share].astype(BF16)
-
-    for blk in range(BLOCKS):
-        for yo in FAR:
-            for zo in FAR:
-                dest = ((my_z + zo) % SIDE) * SIDE + (my_y + yo) % SIDE
-                if not (yo == 0 and zo == 0):
-                    rs_copy(blk, me, dest, my_y, my_z).wait_send()
-
-        @pl.when(sec < last)
-        def _():
+    @pl.when(sec < last)
+    def _():
+        for blk in range(BLOCKS):
+            for zz in range(SIDE):
+                sh_copy(blk, zz, 0).wait_recv()
+        for yy in range(SIDE):
+
+            @pl.when(my_y == yy)
+            def _():
+                whole = jnp.concatenate(
+                    [
+                        sh_buf[blk, zz].astype(F32)
+                        for blk in range(BLOCKS)
+                        for zz in range(SIDE)
+                    ],
+                    axis=0,
+                )
+                sec_out[...] = whole[:, share * yy : share * yy + share].astype(BF16)
+
+    @pl.when(sec < last)
+    def _():
+        for blk in range(BLOCKS):
+            for other in ring[:-1]:
+                rs_copy(blk, me, other, my_y, my_z).wait_send()
             for dest in range(team):
                 ag_copy(blk, me, dest).wait_send()
-
-        for j in range(SIDE):
-
-            @pl.when(my_y * SIDE + j != me)
-            def _():
-                sh_copy(blk, my_z, j).wait_send()
+            for j in range(SIDE):
+
+                @pl.when(my_y * SIDE + j != me)
+                def _():
+                    sh_copy(blk, my_z, j).wait_send()
+
+    @pl.when(sec == last)
+    def _():
+        for blk in range(BLOCKS):
+            for other in ring[:-1]:
+                end_copy(blk, me, other // SIDE, other % SIDE).wait_send()
 
     @pl.when(sec == 0)
     def _():
@@ -621,12 +696,15 @@
             pltpu.VMEM((heads, streams, 128), F32),
             pltpu.VMEM((streams, n_state), F32),
             pltpu.VMEM((pairs, streams, 128), BF16),
-            pltpu.VMEM((128 * pairs, 128), F32),
+            pltpu.VMEM((128 * pairs, streams), BF16),
             pltpu.VMEM((BLOCKS, SIDE, SIDE, rows, chunk + 128), BF16),
             pltpu.VMEM((BLOCKS, team, rows, chunk + 128), BF16),
             pltpu.VMEM((BLOCKS, rows, chunk), BF16),
             pltpu.VMEM((BLOCKS, team, rows, chunk), BF16),
             pltpu.VMEM((BLOCKS, SIDE, rows, chunk), BF16),
+            pltpu.VMEM((BLOCKS, SIDE, SIDE, block, 384), BF16),
+            pltpu.VMEM((BLOCKS, team, block, 384), BF16),
+            pltpu.VMEM((block, 256), F32),
             dma(()),
             dma((1 + heads + SIDE + 1,)),
             dma((len(small),)),

time: 112 us -> 109 us (0.973)
  Pallas kernels: 112 us -> 108 us
    pallas_call x1, Pallas kernels: 109 us -> 106 us  [shards(): pl.pallas_call(functools.partial(kernel, sections), out_shape=(jax.ShapeD...]
where the time goes in v5:
time: 109 us
  Pallas kernels  108 us (99%)
    pallas_call x1, Pallas kernels, shards(): pl.pallas_call(functools.partial(kernel, sections), out_shape=(jax.ShapeD...  106 us
    pallas_call x1, Pallas kernels, shards(): pl.pallas_call(write_out, out_shape=tuple((jax.ShapeDtypeStruct(a.shape,...  2.51 us

profile of v5, /device:TPU:7, one launch (start us, length us, event | category | flops | bytes accessed | tf_op | source)
XLA Modules:
  0.0 108.8 jit_solution(10393837012369033062)
XLA Ops:
  0.6 105.6 %stack_step.1 = (bf16[64,160]{1,0:T(8,128)(2,1)S(1)}, bf16[3,5,64,64]{3,2,1,0:T(8,128)(2,1)S(1)}, bf16[3,64,256]{2,1,0:T(8,128)(2,1)S(1)}, bf16[64,320,128]{2,1,0:T(8,128)(2,1)S(1)}) custom-call(bf16[64,160]{1,0:T(8,128)(2,1)} %hid_hbm.1, f32[1,2560]{1,0:T(1,128)} %gain_hbm.1, bf16[5,2560,128]{2,1,0:T(8,128)(2,1)} %bitcast.30, bf16[2560,256]{1,0:T(8,128)(2,1)} %bitcast.32, ...), custom_call_target="tpu_custom_call" | custom-call | tf_op jit(solution)/shard_map/stack_step/pallas_call | solution.py:669
  106.3 2.5 %write_out.1 = (bf16[64,160]{1,0:T(8,128)(2,1)}, bf16[3,5,64,64]{3,2,1,0:T(8,128)(2,1)}, bf16[3,64,256]{2,1,0:T(8,128)(2,1)}, bf16[64,320,128]{2,1,0:T(8,128)(2,1)}) custom-call(bf16[64,160]{1,0:T(8,128)(2,1)S(1)} %get-tuple-element.12.a_in, bf16[3,5,64,64]{3,2,1,0:T(8,128)(2,1)S(1)} %get-tuple-element.13.b_in, ...), custom_call_target="tpu_custom_call" | custom-call | tf_op jit(solution)/shard_map/write_out/pallas_call | solution.py:726
